TPU v7x, 32 devices: a whole 2x2x4 slice. The times are simulated.
32 devices in a mesh: dp: 8 (over y, x, core), mp: 4 (over z).
Axes of the slice: x: 2, y: 2, z: 4, core: 2. Of those that a mesh axis runs over, the one named last changes fastest.
Arguments:
- tokens: bfloat16 [16384, 768], P(('dp', 'mp')), may hold values from -6 to 6
- segments: int32 [32, 512], P('dp'), may hold values from 0 to 5, never falling along the last dimension, each value on 1 to 256 neighbouring positions
- w_query: bfloat16 [768, 768], P(None, 'mp'), may hold values from -0.21875 to 0.21875
- b_query: bfloat16 [768], P('mp'), may hold values from -3 to 3
- w_key: bfloat16 [768, 768], P(None, 'mp'), may hold values from -0.21875 to 0.21875
- w_value: bfloat16 [768, 768], P(None, 'mp'), may hold values from -0.21875 to 0.21875
- b_value: bfloat16 [768], P('mp'), may hold values from -3 to 3
- w_out: bfloat16 [768, 768], P('mp'), may hold values from -0.625 to 0.625
- b_out: bfloat16 [768], replicated, may hold values from -3 to 3
- first_norm_gain: bfloat16 [768], replicated, may hold values from 0.099609375 to 1.8984375
- first_norm_bias: bfloat16 [768], replicated, may hold values from -3 to 3
- w_up: bfloat16 [768, 3072], P(None, 'mp'), may hold values from -0.21875 to 0.21875
- b_up: bfloat16 [3072], P('mp'), may hold values from -3 to 3
- w_down: bfloat16 [3072, 768], P('mp'), may hold values from -0.109375 to 0.109375
- b_down: bfloat16 [768], replicated, may hold values from -3 to 3
- second_norm_gain: bfloat16 [768], replicated, may hold values from 0.099609375 to 1.8984375
- second_norm_bias: bfloat16 [768], replicated, may hold values from -3 to 3
- output_gradient: bfloat16 [16384, 768], P(('dp', 'mp')), may hold values from -6 to 6
Outputs:
- out_tokens: bfloat16 [16384, 768], P(('dp', 'mp'))
- grad_tokens: bfloat16 [16384, 768], P(('dp', 'mp'))
- grad_w_query: float32 [768, 768], P(None, 'mp')
- grad_b_query: float32 [768], P('mp')
- grad_w_key: float32 [768, 768], P(None, 'mp')
- grad_w_value: float32 [768, 768], P(None, 'mp')
- grad_b_value: float32 [768], P('mp')
- grad_w_out: float32 [768, 768], P('mp')
- grad_b_out: float32 [768], replicated
- grad_norm1_gain: float32 [768], replicated
- grad_norm1_bias: float32 [768], replicated
- grad_w_up: float32 [768, 3072], P(None, 'mp')
- grad_b_up: float32 [3072], P('mp')
- grad_w_down: float32 [3072, 768], P('mp')
- grad_b_down: float32 [768], replicated
- grad_norm2_gain: float32 [768], replicated
- grad_norm2_bias: float32 [768], replicated
Inputs may be any that keep to these rules, and one draw needn't show every extreme that they name: `segments`: document numbers never fall along a sequence; a document holds 1 to 256 positions, and in every sequence one holds exactly 256.
All inputs are finite; a program needn't handle non-finite values.
Results may differ from a plain program's by a relative error of at most 0.015.
Values may be sent and summed in bfloat16 or wider, within the bound.
No kernel may reach another device: no remote copies, remote signals or barrier semaphores. Data moves between devices by JAX's collectives and lax.ppermute only.
A program may use at most 128 MiB of HBM per device.

v0:
```python
import jax
import jax.numpy as jnp
from jax import lax
from jax.sharding import PartitionSpec as P

HEAD_DIM = 64


EPS = 1e-05
INV_ROOT_TWO = 0.7071067811865476
INV_ROOT_TWO_PI = 0.3989422804014327


def matmul(left, right):
    return jnp.dot(left, right, preferred_element_type=jnp.float32)


def left_transposed(left, right):
    return lax.dot_general(
        left, right, (((0,), (0,)), ((), ())), preferred_element_type=jnp.float32
    )


def right_transposed(left, right):
    return lax.dot_general(
        left, right, (((1,), (1,)), ((), ())), preferred_element_type=jnp.float32
    )


def row_product(left, right):
    return matmul(left, right)


def layer_norm_forward(values, gain_vector, bias_vector):
    average = jnp.mean(values, -1, keepdims=True)
    centered_rows = values - average
    spread = jnp.mean(centered_rows * centered_rows, -1, keepdims=True)
    inverse_deviation = lax.rsqrt(spread + EPS)
    standardized_rows = centered_rows * inverse_deviation
    return (
        standardized_rows * gain_vector.astype(jnp.float32) + bias_vector.astype(jnp.float32),
        standardized_rows,
        inverse_deviation,
    )


def layer_norm_backward(incoming_gradient, standardized_rows, inverse_deviation, gain_vector):
    scaled_rows = incoming_gradient * gain_vector.astype(jnp.float32)
    layer_result = inverse_deviation * (
        scaled_rows
        - jnp.mean(scaled_rows, -1, keepdims=True)
        - standardized_rows * jnp.mean(scaled_rows * standardized_rows, -1, keepdims=True)
    )
    return (
        layer_result,
        jnp.sum(incoming_gradient * standardized_rows, 0),
        jnp.sum(incoming_gradient, 0),
    )


def gelu_slope(values):
    return (
        0.5 * (1.0 + lax.erf(values * INV_ROOT_TWO))
        + values * jnp.exp(-0.5 * values * values) * INV_ROOT_TWO_PI
    )


def masked_scores(queries, key_rows, segment):
    scores = jnp.einsum(
        "qhd,khd->hqk", queries, key_rows, preferred_element_type=jnp.float32
    ) * HEAD_DIM ** (-0.5)
    same_doc = segment[:, None] == segment[None, :]
    return jnp.where(same_doc[None], scores, -1e30)


def attend_forward(blocks):
    queries, key_rows, value_rows, segment = blocks
    scores = masked_scores(queries, key_rows, segment)
    highest = jnp.max(scores, -1, keepdims=True)
    expd = jnp.exp(scores - highest)
    totals = jnp.sum(expd, -1, keepdims=True)
    attn_probs = (expd / totals).astype(jnp.bfloat16)
    context = jnp.einsum("hqk,khd->qhd", attn_probs, value_rows, preferred_element_type=jnp.float32)
    return (context.astype(jnp.bfloat16), (highest + jnp.log(totals))[..., 0])


def attend_backward(blocks):
    queries, key_rows, value_rows, g_context, log_sums, segment = blocks
    scores = masked_scores(queries, key_rows, segment)
    attn_probs = jnp.exp(scores - log_sums[..., None])
    g_value = jnp.einsum(
        "hqk,qhd->khd",
        attn_probs.astype(jnp.bfloat16),
        g_context,
        preferred_element_type=jnp.float32,
    )
    g_probs = jnp.einsum("qhd,khd->hqk", g_context, value_rows, preferred_element_type=jnp.float32)
    centre = jnp.sum(attn_probs * g_probs, -1, keepdims=True)
    g_scores = (attn_probs * (g_probs - centre)).astype(jnp.bfloat16)
    scale = HEAD_DIM ** (-0.5)
    g_query = scale * jnp.einsum(
        "hqk,khd->qhd", g_scores, key_rows, preferred_element_type=jnp.float32
    )
    g_key = scale * jnp.einsum(
        "hqk,qhd->khd", g_scores, queries, preferred_element_type=jnp.float32
    )
    return (g_query.astype(jnp.bfloat16), g_key.astype(jnp.bfloat16), g_value.astype(jnp.bfloat16))


def input_terms(g_query, g_key, g_value, w_query, w_key, w_value):
    total = right_transposed(g_query, w_query)
    total = total + right_transposed(g_key, w_key)
    return total + right_transposed(g_value, w_value)


def hidden_terms(g_pre, w_up):
    return right_transposed(g_pre, w_up)


def per_device(
    tokens,
    segments,
    w_query,
    b_query,
    w_key,
    w_value,
    b_value,
    w_out,
    b_out,
    first_norm_gain,
    first_norm_bias,
    w_up,
    b_up,
    w_down,
    b_down,
    second_norm_gain,
    second_norm_bias,
    output_gradient,
):
    seq_count = segments.shape[0]
    seq_len = segments.shape[1]
    heads_here = w_query.shape[1] // HEAD_DIM
    full_tokens = lax.all_gather(tokens, "mp", axis=0, tiled=True)
    queries = (matmul(full_tokens, w_query) + b_query.astype(jnp.float32)).astype(jnp.bfloat16)
    key_rows = matmul(full_tokens, w_key).astype(jnp.bfloat16)
    value_rows = (matmul(full_tokens, w_value) + b_value.astype(jnp.float32)).astype(jnp.bfloat16)

    def by_head(tensor):
        return tensor.reshape(seq_count, seq_len, heads_here, HEAD_DIM)

    def by_rows(tensor):
        return tensor.reshape(seq_count * seq_len, heads_here * HEAD_DIM)

    context, log_sums = lax.map(
        attend_forward, (by_head(queries), by_head(key_rows), by_head(value_rows), segments)
    )
    context = by_rows(context)
    attn_part = lax.psum_scatter(row_product(context, w_out), "mp", scatter_dimension=0, tiled=True)
    attention_output = tokens.astype(jnp.float32) + attn_part + b_out.astype(jnp.float32)
    normalized_rows, standardized_first, inverse_deviation_first = layer_norm_forward(
        attention_output, first_norm_gain, first_norm_bias
    )
    full_normed = lax.all_gather(normalized_rows.astype(jnp.bfloat16), "mp", axis=0, tiled=True)
    pre_act = matmul(full_normed, w_up) + b_up.astype(jnp.float32)
    activated = jax.nn.gelu(pre_act, approximate=False).astype(jnp.bfloat16)
    ffn_part = lax.psum_scatter(
        row_product(activated, w_down), "mp", scatter_dimension=0, tiled=True
    )
    residual_sum = normalized_rows + ffn_part + b_down.astype(jnp.float32)
    output_rows, standardized_second, inverse_deviation_second = layer_norm_forward(
        residual_sum, second_norm_gain, second_norm_bias
    )
    summed_gradient, grad_gain_two, grad_bias_two = layer_norm_backward(
        output_gradient.astype(jnp.float32),
        standardized_second,
        inverse_deviation_second,
        second_norm_gain,
    )
    grad_b_down = jnp.sum(summed_gradient, 0)
    full_g_summed = lax.all_gather(summed_gradient.astype(jnp.bfloat16), "mp", axis=0, tiled=True)
    grad_w_down = left_transposed(activated, full_g_summed)
    g_pre = (right_transposed(full_g_summed, w_down) * gelu_slope(pre_act)).astype(jnp.bfloat16)
    grad_w_up = left_transposed(full_normed, g_pre)
    grad_b_up = jnp.sum(g_pre.astype(jnp.float32), 0)
    hidden_slice = lax.psum_scatter(
        hidden_terms(g_pre, w_up), "mp", scatter_dimension=0, tiled=True
    )
    g_attended, grad_gain_one, grad_bias_one = layer_norm_backward(
        summed_gradient + hidden_slice, standardized_first, inverse_deviation_first, first_norm_gain
    )
    grad_b_out = jnp.sum(g_attended, 0)
    full_g_attended = lax.all_gather(g_attended.astype(jnp.bfloat16), "mp", axis=0, tiled=True)
    grad_w_out = left_transposed(context, full_g_attended)
    g_context = right_transposed(full_g_attended, w_out).astype(jnp.bfloat16)
    g_query, g_key, g_value = lax.map(
        attend_backward,
        (
            by_head(queries),
            by_head(key_rows),
            by_head(value_rows),
            by_head(g_context),
            log_sums,
            segments,
        ),
    )
    g_query = by_rows(g_query)
    g_key = by_rows(g_key)
    g_value = by_rows(g_value)
    grad_w_query = left_transposed(full_tokens, g_query)
    grad_w_key = left_transposed(full_tokens, g_key)
    grad_w_value = left_transposed(full_tokens, g_value)
    grad_b_query = jnp.sum(g_query.astype(jnp.float32), 0)
    grad_b_value = jnp.sum(g_value.astype(jnp.float32), 0)
    input_part = lax.psum_scatter(
        input_terms(g_query, g_key, g_value, w_query, w_key, w_value).astype(jnp.bfloat16),
        "mp",
        scatter_dimension=0,
        tiled=True,
    ).astype(jnp.float32)
    grad_rows = (g_attended + input_part).astype(jnp.bfloat16)
    (
        grad_w_query,
        grad_b_query,
        grad_w_key,
        grad_w_value,
        grad_b_value,
        grad_w_out,
        grad_w_up,
        grad_b_up,
        grad_w_down,
    ) = lax.psum(
        (
            grad_w_query,
            grad_b_query,
            grad_w_key,
            grad_w_value,
            grad_b_value,
            grad_w_out,
            grad_w_up,
            grad_b_up,
            grad_w_down,
        ),
        "dp",
    )
    grad_gain_one, grad_bias_one, grad_gain_two, grad_bias_two, grad_b_down, grad_b_out = lax.psum(
        (grad_gain_one, grad_bias_one, grad_gain_two, grad_bias_two, grad_b_down, grad_b_out),
        ("dp", "mp"),
    )
    return (
        output_rows.astype(jnp.bfloat16),
        grad_rows,
        grad_w_query,
        grad_b_query,
        grad_w_key,
        grad_w_value,
        grad_b_value,
        grad_w_out,
        grad_b_out,
        grad_gain_one,
        grad_bias_one,
        grad_w_up,
        grad_b_up,
        grad_w_down,
        grad_b_down,
        grad_gain_two,
        grad_bias_two,
    )


def solution(mesh):
    in_specs = (
        P(("dp", "mp"), None),
        P("dp", None),
        P(None, "mp"),
        P("mp"),
        P(None, "mp"),
        P(None, "mp"),
        P("mp"),
        P("mp", None),
        P(),
        P(),
        P(),
        P(None, "mp"),
        P("mp"),
        P("mp", None),
        P(),
        P(),
        P(),
        P(("dp", "mp"), None),
    )
    out_specs = (
        P(("dp", "mp"), None),
        P(("dp", "mp"), None),
        P(None, "mp"),
        P("mp"),
        P(None, "mp"),
        P(None, "mp"),
        P("mp"),
        P("mp", None),
        P(),
        P(),
        P(),
        P(None, "mp"),
        P("mp"),
        P("mp", None),
        P(),
        P(),
        P(),
    )
    return jax.shard_map(
        per_device, mesh=mesh, in_specs=in_specs, out_specs=out_specs, check_vma=False
    )
```

profile of v0, /device:TPU:0, one launch (start us, length us, event | category | flops | bytes accessed | tf_op | source)
XLA Modules:
  0.0 936.5 jit_solution(3617717187494992578)
XLA Ops:
  9.3 66.5 %all-gather.5.cloned.1.call-done = bf16[2048,768]{1,0:T(8,128)(2,1)} async-done(((bf16[512,768]{1,0:T(8,128)(2,1)}), bf16[2048,768]{1,0:T(8,128)(2,1)}) %all-gather.5.cloned.1.call-update) | async-done | bytes 3145744 | tf_op jit(solution)/shard_map/all_gather | solution.py:143
  75.8 3.1 fusion.70
  79.7 3.1 fusion.71
  83.5 3.1 convolution_convert_fusion.1
  90.3 19.1 %while.26 = (s32[]{:T(128)}, bf16[4,512,3,64]{1,3,2,0:T(8,128)(2,1)}, f32[4,3,512]{2,1,0:T(4,128)}, bf16[4,512,3,64]{1,3,2,0:T(8,128)(2,1)S(1)}, s32[4,512]{1,0:...) while((s32[]{:T(128)}, ...), condition=%wide.region_3.4_spmd, body=%wide.region_0.3_spmd.sunk | while | flops 211122688 | bytes 11335781 | solution.py:154
  92.7 1.8 fusion.150
  97.4 1.8 fusion.150
  102.2 1.8 fusion.150
  107.0 1.8 fusion.150
  109.4 2.3 copy.53
  112.8 3.7 fusion.85
  117.2 108.9 %reduce-scatter.5.cloned.1.call-done = f32[512,768]{1,0:T(8,128)} async-done(((f32[2048,768]{1,0:T(8,128)}), f32[512,768]{1,0:T(8,128)}) %reduce-scatter.5.cloned.1.call-update) | async-done | bytes 1572880 | tf_op jit(solution)/shard_map/reduce_scatter | solution.py:158
  226.1 1.9 fusion.84
  231.0 62.7 %all-gather.7.cloned.1.call-done = bf16[2048,768]{1,0:T(8,128)(2,1)} async-done(((bf16[512,768]{1,0:T(8,128)(2,1)}), bf16[2048,768]{1,0:T(8,128)(2,1)}) %all-gather.7.cloned.1.call-update) | async-done | bytes 3145744 | tf_op jit(solution)/shard_map/all_gather | solution.py:163
  293.7 17.9 %fusion.56 = (bf16[2048,768]{1,0:T(8,128)(2,1)S(1)}, f32[2048,768]{1,0:T(8,128)}) fusion(f32[768]{0:T(1024)} %convert_element_type.128, bf16[2048,768]{1,0:T(8,128)(2,1)} %all-gather.7.cloned.1.call-done, bf16[768,768]{1,0:T(8,128)(2,1)S(1)} %copy-done), kind=kOutput, calls=%fused_computation.66 | convolution fusion | flops 2519728128 | bytes 13765632 | tf_op jit(solution)/shard_map/dot_general | solution.py:15
  311.5 1.7 copy-done.37
  313.2 4.4 fusion.86
  321.5 105.7 %reduce-scatter.7.cloned.1.call-done = f32[512,768]{1,0:T(8,128)} async-done(((f32[2048,768]{1,0:T(8,128)}), f32[512,768]{1,0:T(8,128)}) %reduce-scatter.7.cloned.1.call-update) | async-done | bytes 1572880 | tf_op jit(solution)/shard_map/reduce_scatter | solution.py:166
  427.2 2.1 fusion.83
  431.0 2.1 fusion.80
  435.3 64.1 %all-gather.9.cloned.1.call-done = bf16[2048,768]{1,0:T(8,128)(2,1)} async-done(((bf16[512,768]{1,0:T(8,128)(2,1)}), bf16[2048,768]{1,0:T(8,128)(2,1)}) %all-gather.9.cloned.1.call-update) | async-done | bytes 3145744 | tf_op jit(solution)/shard_map/all_gather | solution.py:180
  499.4 7.5 convert_reduce_fusion
  506.9 1.6 copy-done.38
  508.6 4.5 fusion.87
  513.2 109.5 %reduce-scatter.9.cloned.1.call-done = f32[512,768]{1,0:T(8,128)} async-done(((f32[2048,768]{1,0:T(8,128)}), f32[512,768]{1,0:T(8,128)}) %reduce-scatter.9.cloned.1.call-update) | async-done | bytes 1572880 | tf_op jit(solution)/shard_map/reduce_scatter | solution.py:185
  622.7 3.3 multiply_reduce_fusion.1
  629.5 63.9 %all-gather.11.cloned.1.call-done = bf16[2048,768]{1,0:T(8,128)(2,1)} async-done(((bf16[512,768]{1,0:T(8,128)(2,1)}), bf16[2048,768]{1,0:T(8,128)(2,1)}) %all-gather.11.cloned.1.call-update) | async-done | bytes 3145744 | tf_op jit(solution)/shard_map/all_gather | solution.py:192
  693.5 3.1 convolution_convert_fusion
  699.3 32.5 %while.27 = (s32[]{:T(128)}, bf16[4,512,3,64]{1,3,2,0:T(8,128)(2,1)}, bf16[4,512,3,64]{1,3,2,0:T(8,128)(2,1)}, bf16[4,512,3,64]{1,3,2,0:T(8,128)(2,1)S(1)}, bf16...) while((s32[]{:T(128)}, ...), condition=%wide.region_17.18_spmd, body=%wide.region_15.17_spmd.sunk | while | flops 511146496 | bytes 26127484 | solution.py:195
  700.9 1.5 fusion.159
  709.0 1.5 fusion.159
  717.1 1.5 fusion.159
  725.3 1.5 fusion.159
  731.8 2.1 copy.59
  737.8 2.8 add_convert_fusion
  740.9 7.1 fusion.92
  748.0 4.2 fusion.91
  752.2 1.6 fusion.90
  754.3 1.6 convolution_bitcast_fusion.2
  755.9 1.6 convolution_bitcast_fusion
  757.5 1.6 convolution_bitcast_fusion.1
  759.9 44.8 %all-reduce = (f32[768]{0:T(1024)}, f32[768]{0:T(1024)}, f32[768]{0:T(1024)}, f32[768]{0:T(1024)}, f32[768]{0:T(1024)}, /*index=5*/f32[768]{0:T(1024)}) all-reduce(f32[768]{0:T(1024)S(1)} %copy-done.26, f32[768]{0:T(1024)S(1)} %copy-done.29, f32[768]{0:T(1024)S(1)} %copy-done.30, ...), channel_id=1, replica_groups=mesh['dp'=8,'mp'=4] {'dp','mp'}, use_global_device_ids=true, to_apply=%region_28.29 | all-reduce | flops 4608 | bytes 36864 | tf_op jit(solution)/shard_map/psum | solution.py:245
  805.2 14.2 %all-reduce.1 = (f32[192]{0:T(256)}, f32[192]{0:T(256)}, f32[768]{0:T(1024)}) all-reduce(f32[192]{0:T(256)S(1)} %reduce_sum.184, f32[192]{0:T(256)S(1)} %reduce_sum.186, f32[768]{0:T(1024)S(1)} %copy-done.31), channel_id=1, replica_groups=mesh['dp'=8,'mp'=4] {'dp'}, use_global_device_ids=true, to_apply=%region_21.22 | all-reduce | flops 1152 | bytes 9216 | tf_op jit(solution)/shard_map/psum | solution.py:231
  819.5 2.2 add_convert_fusion.1
  821.7 98.3 %all-reduce.5.cloned.1.call-done = (f32[768,192]{0,1:T(8,128)}, f32[768,192]{0,1:T(8,128)}, f32[768,192]{0,1:T(8,128)}, f32[192,768]{1,0:T(8,128)}, f32[768,768]{1,0:T(8,128)}, /*index=5*/f32[768,768]{1,0:T(8,128)}) async-done(((f32[768,192]{0,1:T(8,128)}, f32[768,192]{0,1:T(8,128)}, f32[768,192]{0,1:T(8,128)}, f32[192,768]{1,0:T(8,128)}, f32[768,768]{1,0:T(8,128)}, /*index=5*/f32[768,768]{1,0:T(8,128)}), ...) | async-done | bytes 7077904 | tf_op jit(solution)/shard_map/psum | solution.py:231
  920.0 2.1 copy.103
  922.1 1.9 copy.104
  924.0 1.9 copy.105
  (200 shorter events, 73.8 us)
Async XLA Ops:
  7.2 286.5 %copy-start = (bf16[768,768]{1,0:T(8,128)(2,1)S(1)}, bf16[768,768]{1,0:T(8,128)(2,1)}, u32[]{:S(2)}) copy-start(bf16[768,768]{1,0:T(8,128)(2,1)} %param.33) | copy-start | bytes 3538948
  7.2 68.6 %all-gather.5.cloned.1.call-start = ((), (), s32[]{:S(2)}) async-start(), calls=%async_computation.4 | async-start | bytes 3932160 | tf_op jit(solution)/shard_map/all_gather | solution.py:143
  7.9 218.1 %reduce-scatter.5.cloned.1.call-start = ((), (), s32[]{:S(2)}) async-start(), calls=%async_computation.5 | async-start | bytes 7864320 | tf_op jit(solution)/shard_map/reduce_scatter | solution.py:158
  109.4 7.1 copy-start.3
  109.4 7.1 copy-start.13
  109.4 3.4 copy-start.19
  111.9 0.9 copy-start.8
  116.5 0.7 copy-start.33
  116.5 0.7 copy-start.34
  116.5 177.2 %all-gather.7.cloned.1.call-start = ((), (), s32[]{:S(2)}) async-start(), calls=%async_computation.6 | async-start | bytes 3932160 | tf_op jit(solution)/shard_map/all_gather | solution.py:163
  229.5 197.7 %reduce-scatter.7.cloned.1.call-start = ((), (), s32[]{:S(2)}) async-start(), calls=%async_computation.7 | async-start | bytes 7864320 | tf_op jit(solution)/shard_map/reduce_scatter | solution.py:166
  293.7 19.5 %copy-start.36 = (bf16[768,768]{1,0:T(8,128)(2,1)S(1)}, bf16[768,768]{1,0:T(8,128)(2,1)}, u32[]{:S(2)}) copy-start(bf16[768,768]{1,0:T(8,128)(2,1)} %param.35) | copy-start | bytes 3538948
  311.5 1.7 copy-start.37
  317.7 181.8 %all-gather.9.cloned.1.call-start = ((), (), s32[]{:S(2)}) async-start(), calls=%async_computation.8 | async-start | bytes 3932160 | tf_op jit(solution)/shard_map/all_gather | solution.py:180
  427.2 2.4 copy-start.15
  427.2 2.4 copy-start.24
  429.3 1.7 copy-start.27
  433.1 1.1 copy-start.7
  435.2 187.4 %reduce-scatter.9.cloned.1.call-start = ((), (), s32[]{:S(2)}) async-start(), calls=%async_computation.9 | async-start | bytes 7864320 | tf_op jit(solution)/shard_map/reduce_scatter | solution.py:185
  506.9 1.6 copy-start.38
  513.1 180.3 %all-gather.11.cloned.1.call-start = ((), (), s32[]{:S(2)}) async-start(), calls=%async_computation.10 | async-start | bytes 3932160 | tf_op jit(solution)/shard_map/all_gather | solution.py:192
  626.0 67.5 %copy-start.20 = (bf16[192,768]{1,0:T(8,128)(2,1)S(1)}, bf16[192,768]{1,0:T(8,128)(2,1)}, u32[]{:S(2)}) copy-start(bf16[192,768]{1,0:T(8,128)(2,1)} %param.29) | copy-start | bytes 884740
  627.1 1.2 copy-start.5
  629.3 190.2 %reduce-scatter.11.cloned.1.call-start = ((), (), s32[]{:S(2)}) async-start(), calls=%async_computation.11 | async-start | bytes 3932160 | tf_op jit(solution)/shard_map/reduce_scatter | solution.py:214
  696.5 2.7 copy-start.4
  731.8 2.9 copy-start.10
  731.8 3.1 copy-start.12
  734.0 1.6 copy-start.21
  735.7 1.1 copy-start.22
  736.7 1.1 copy-start.23
  740.6 179.4 %all-reduce.5.cloned.1.call-start = ((), (), s32[]{:S(2)}) async-start(), calls=%async_computation.12 | async-start | bytes 14155776 | tf_op jit(solution)/shard_map/psum | solution.py:231
  740.9 7.1 copy-start.35
  740.9 7.1 copy-start.39
  748.0 4.2 copy-start.9
  748.0 4.2 copy-start.14
  752.2 2.2 copy-start.2
  759.1 0.7 copy-start.25
  759.1 0.7 copy-start.26
  759.1 0.7 copy-start.28
  759.1 0.7 copy-start.29
  759.1 0.7 copy-start.30
  759.1 45.5 %copy-start.11 = (bf16[4,512,3,64]{1,3,2,0:T(8,128)(2,1)S(1)}, bf16[4,512,3,64]{1,3,2,0:T(8,128)(2,1)}, u32[]{:S(2)}) copy-start(bf16[4,512,3,64]{1,3,2,0:T(8,128)(2,1)} %copy-done.10) | copy-start | bytes 2359300
  759.1 46.1 %copy-start.31 = (f32[768]{0:T(1024)S(1)}, f32[768]{0:T(1024)}, u32[]{:S(2)}) copy-start(f32[768]{0:T(1024)} %get-tuple-element.221) | copy-start | bytes 9220
  759.2 60.3 %copy-start.6 = (f32[512,768]{1,0:T(8,128)S(1)}, f32[512,768]{1,0:T(8,128)}, u32[]{:S(2)}) copy-start(f32[512,768]{1,0:T(8,128)} %copy-done.5) | copy-start | bytes 4718596
  920.0 5.9 copy-start.18
  920.0 6.7 copy-start.17
  925.9 2.2 copy-start.16
  926.7 2.8 copy-start.1
  (1 other events, 0.7 us)
Sparse Core Ops, SparseCore 0:
  9.6 66.1 all-gather.4
  116.6 109.3 reduce-scatter.4
  229.6 64.0 all-gather.6
  317.8 109.3 reduce-scatter.6
  435.4 64.0 all-gather.8
  513.2 109.3 reduce-scatter.8
  629.4 64.0 all-gather.10
  740.7 59.9 reduce-scatter.10
  805.9 114.0 all-reduce.4
where the time goes:
time: 945 us; the launch traced here: 937 us
  waiting for transfers between devices  680 us (72%)
  matrix products  106 us (11%)
  blocking collectives  59 us (6%)
  local copies, waits for them, and re-layouts  40.7 us (4%)
  other arithmetic  34.8 us (4%)
  between operations  14.7 us (2%)
    reduce_scatter x1, waiting for transfers between devices, per_device(): lax.psum_scatter(hidden_terms(g_pre, w_up), 'mp', scatter_dimension=0, ti...  110 us
    reduce_scatter x1, waiting for transfers between devices, per_device(): lax.psum_scatter(row_product(context, w_out), 'mp', scatter_dimension=0,...  109 us
    reduce_scatter x1, waiting for transfers between devices, per_device(): lax.psum_scatter(row_product(activated, w_down), 'mp', scatter_dimension=...  106 us
    psum x1, waiting for transfers between devices, per_device(): lax.psum((grad_w_query, grad_b_query, grad_w_key, grad_w_value, grad_b_va...  98.3 us
    all_gather x1, waiting for transfers between devices, per_device(): full_tokens = lax.all_gather(tokens, 'mp', axis=0, tiled=True)  66.5 us
    all_gather x1, waiting for transfers between devices, per_device(): lax.all_gather(summed_gradient.astype(jnp.bfloat16), 'mp', axis=0, tiled=...  64.1 us
    all_gather x1, waiting for transfers between devices, per_device(): lax.all_gather(g_attended.astype(jnp.bfloat16), 'mp', axis=0, tiled=True)  63.9 us
    all_gather x1, waiting for transfers between devices, per_device(): lax.all_gather(normalized_rows.astype(jnp.bfloat16), 'mp', axis=0, tiled=...  62.7 us
  transfers between devices with their start and end apart: 9, of which 8 were waited for; matrix products, arithmetic and copies ran while one was open for 3% of the time, Pallas kernels for 0%

commit v1 on v0

v1 whole, which is shorter than its diff:
```python
import jax
import jax.numpy as jnp
from jax import lax
from jax.sharding import PartitionSpec as P

HEAD_DIM = 64
EPS = 1e-05
INV_ROOT_TWO = 0.7071067811865476
INV_ROOT_TWO_PI = 0.3989422804014327
CUBE = 8

f32 = jnp.float32
bf16 = jnp.bfloat16


def dot(left, right, dims):
    return lax.dot_general(left, right, ((dims[:1], dims[1:]), ((), ())), preferred_element_type=f32)


def norm_forward(values, gain, bias):
    average = jnp.mean(values, -1, keepdims=True)
    centered = values - average
    spread = jnp.mean(centered * centered, -1, keepdims=True)
    rstd = lax.rsqrt(spread + EPS)
    xhat = centered * rstd
    return xhat * gain + bias, xhat, rstd


def norm_backward(grad, xhat, rstd, gain):
    scaled = grad * gain
    result = rstd * (
        scaled
        - jnp.mean(scaled, -1, keepdims=True)
        - xhat * jnp.mean(scaled * xhat, -1, keepdims=True)
    )
    return result, jnp.sum(grad * xhat, 0), jnp.sum(grad, 0)


def gelu_parts(v):
    phi = 0.5 * (1.0 + lax.erf(v * INV_ROOT_TWO))
    return v * phi, phi + v * jnp.exp(-0.5 * v * v) * INV_ROOT_TWO_PI


class Links:
    def __init__(self, dp, mp):
        self.dp, self.mp = dp, mp
        self.index = lax.axis_index("dp")
        self.place = self.index % CUBE

    def shift(self, x, by):
        return lax.ppermute(x, "mp", [(i, (i + by) % self.mp) for i in range(self.mp)])

    def flip(self, x, bit):
        return lax.ppermute(x, "dp", [(i, i ^ bit) for i in range(self.dp)])

    def spread(self, piece):
        half = piece.shape[0] // 2
        over_x = self.flip(piece, 2)
        over_y = self.flip(piece, 4)
        diag_a = self.flip(over_x[:half], 4)
        diag_b = self.flip(over_y[half:], 2)
        diag = jnp.concatenate([diag_a, diag_b])
        even = [piece, over_x, over_y, diag]
        odd = [self.flip(part, 1) for part in even]
        return [even[0], odd[0], even[1], odd[1], even[2], odd[2], even[3], odd[3]]

    def ordered(self, parts):
        stacked = jnp.stack(parts)
        return jnp.stack(
            [
                lax.dynamic_index_in_dim(stacked, self.place ^ q, 0, keepdims=False)
                for q in range(CUBE)
            ]
        )

    def gather(self, shard):
        rows, cols = shard.shape
        step = rows // CUBE
        piece = lax.dynamic_slice_in_dim(shard, self.place * step, step, 0)
        others = jnp.concatenate([self.shift(piece, s) for s in range(1, self.mp)])
        whole = self.ordered(self.spread(others)).reshape(CUBE, self.mp - 1, step, cols)
        whole = whole.transpose(1, 0, 2, 3).reshape(self.mp - 1, rows, cols)
        return [shard] + [whole[s] for s in range(self.mp - 1)]

    def reduce(self, blocks):
        rows, cols = blocks[0].shape
        step = rows // CUBE
        stacked = jnp.stack(blocks).reshape(self.mp, CUBE, step, cols)
        rel = [
            lax.dynamic_index_in_dim(stacked, self.place ^ r, 1, keepdims=False).astype(bf16)
            for r in range(CUBE)
        ]
        other = self.flip(jnp.stack(rel[1::2]), 1)
        add = lambda *terms: sum(t.astype(f32) for t in terms).astype(bf16)
        own, to_x, to_y, to_diag = [add(rel[2 * i], other[i]) for i in range(4)]
        cut = self.mp // 2
        a, b = slice(0, cut), slice(cut, self.mp)
        from_x = self.flip(jnp.stack([to_diag[a], to_x[a]]), 2)
        from_y = self.flip(jnp.stack([to_diag[b], to_y[b]]), 4)
        last_x = self.flip(add(to_x[b], from_y[0]), 2)
        last_y = self.flip(add(to_y[a], from_x[0]), 4)
        own = jnp.concatenate([add(own[a], from_x[1], last_y), add(own[b], last_x, from_y[1])])
        terms = [own[0]] + [self.shift(own[s], -s) for s in range(1, self.mp)]
        total = sum(t.astype(f32) for t in terms)
        if self.dp > CUBE:
            groups = [[g * CUBE + i for g in range(self.dp // CUBE)] for i in range(CUBE)]
            total = lax.psum(total, "dp", axis_index_groups=groups)
        return total


def scores_of(queries, key_rows, same_doc):
    scores = jnp.einsum("qhd,khd->hqk", queries, key_rows, preferred_element_type=f32)
    return jnp.where(same_doc[None], scores * HEAD_DIM ** (-0.5), -1e30)


def attend_forward(queries, key_rows, value_rows, same_doc):
    scores = scores_of(queries, key_rows, same_doc)
    highest = jnp.max(scores, -1, keepdims=True)
    expd = jnp.exp(scores - highest)
    totals = jnp.sum(expd, -1, keepdims=True)
    probs = (expd / totals).astype(bf16)
    context = jnp.einsum("hqk,khd->qhd", probs, value_rows, preferred_element_type=f32)
    return context.astype(bf16), (highest + jnp.log(totals))[..., 0]


def attend_backward(queries, key_rows, value_rows, g_context, log_sums, same_doc):
    scores = scores_of(queries, key_rows, same_doc)
    probs = jnp.exp(scores - log_sums[..., None])
    g_value = jnp.einsum("hqk,qhd->khd", probs.astype(bf16), g_context, preferred_element_type=f32)
    g_probs = jnp.einsum("qhd,khd->hqk", g_context, value_rows, preferred_element_type=f32)
    centre = jnp.sum(probs * g_probs, -1, keepdims=True)
    g_scores = (probs * (g_probs - centre)).astype(bf16)
    scale = HEAD_DIM ** (-0.5)
    g_query = scale * jnp.einsum("hqk,khd->qhd", g_scores, key_rows, preferred_element_type=f32)
    g_key = scale * jnp.einsum("hqk,qhd->khd", g_scores, queries, preferred_element_type=f32)
    return g_query.astype(bf16), g_key.astype(bf16), g_value.astype(bf16)


def per_device(
    dp,
    mp,
    tokens,
    segments,
    w_query,
    b_query,
    w_key,
    w_value,
    b_value,
    w_out,
    b_out,
    first_norm_gain,
    first_norm_bias,
    w_up,
    b_up,
    w_down,
    b_down,
    second_norm_gain,
    second_norm_bias,
    output_gradient,
):
    links = Links(dp, mp)
    slots = range(mp)
    rows, width = tokens.shape
    part = w_query.shape[1]
    heads = part // HEAD_DIM
    gain1, bias1 = first_norm_gain.astype(f32), first_norm_bias.astype(f32)
    gain2, bias2 = second_norm_gain.astype(f32), second_norm_bias.astype(f32)
    segment = lax.dynamic_index_in_dim(segments, lax.axis_index("mp"), 0, keepdims=False)
    same_doc = segment[:, None] == segment[None, :]

    mixed = jnp.concatenate([w_query, w_key, w_value, w_out.T], axis=1)
    a_blocks = links.gather(mixed)
    vectors = jnp.concatenate([b_query, b_value, b_up])
    vectors = [vectors] + [links.shift(vectors, s) for s in range(1, mp)]
    bq = [v[:part].astype(f32) for v in vectors]
    bv = [v[part : 2 * part].astype(f32) for v in vectors]
    bu = [v[2 * part :].astype(f32) for v in vectors]
    u_blocks = links.gather(w_up)
    d_blocks = links.gather(w_down)

    by_head = lambda t: t.reshape(rows, heads, HEAD_DIM)
    by_rows = lambda t: t.reshape(rows, heads * HEAD_DIM)
    saved = []
    attended = tokens.astype(f32) + b_out.astype(f32)
    for s in slots:
        mix = dot(tokens, a_blocks[s][:, : 3 * part], (1, 0))
        q = by_head((mix[:, :part] + bq[s]).astype(bf16))
        k = by_head(mix[:, part : 2 * part].astype(bf16))
        v = by_head((mix[:, 2 * part :] + bv[s]).astype(bf16))
        context, sums = attend_forward(q, k, v, same_doc)
        context = by_rows(context)
        saved.append((q, k, v, context, sums))
        attended = attended + dot(context, a_blocks[s][:, 3 * part :], (1, 1))
    normed, xhat1, rstd1 = norm_forward(attended, gain1, bias1)
    normed_low = normed.astype(bf16)
    acts, slopes = [], []
    summed = normed + b_down.astype(f32)
    for s in slots:
        act, slope = gelu_parts(dot(normed_low, u_blocks[s], (1, 0)) + bu[s])
        acts.append(act.astype(bf16))
        slopes.append(slope)
        summed = summed + dot(acts[s], d_blocks[s], (1, 0))
    out_tokens, xhat2, rstd2 = norm_forward(summed, gain2, bias2)
    g_summed, g_gain2, g_bias2 = norm_backward(output_gradient.astype(f32), xhat2, rstd2, gain2)
    g_b_down = jnp.sum(g_summed, 0)
    g_low = g_summed.astype(bf16)
    piece_d = links.reduce([dot(acts[s], g_low, (0, 0)) for s in slots])
    g_pre = [(dot(g_low, d_blocks[s], (1, 1)) * slopes[s]).astype(bf16) for s in slots]
    piece_u = links.reduce([dot(normed_low, g_pre[s], (0, 0)) for s in slots])
    g_b_up = [jnp.sum(g.astype(f32), 0) for g in g_pre]
    g_normed = g_summed
    for s in slots:
        g_normed = g_normed + dot(g_pre[s], u_blocks[s], (1, 1))
    g_attended, g_gain1, g_bias1 = norm_backward(g_normed, xhat1, rstd1, gain1)
    g_b_out = jnp.sum(g_attended, 0)
    ga_low = g_attended.astype(bf16)
    g_tokens = g_attended
    g_mixed, g_bq, g_bv = [], [], []
    for s in slots:
        q, k, v, context, sums = saved[s]
        g_out = dot(ga_low, context, (0, 0))
        g_context = by_head(dot(ga_low, a_blocks[s][:, 3 * part :], (1, 0)).astype(bf16))
        gq, gk, gv = attend_backward(q, k, v, g_context, sums, same_doc)
        gq, gk, gv = by_rows(gq), by_rows(gk), by_rows(gv)
        g_bq.append(jnp.sum(gq.astype(f32), 0))
        g_bv.append(jnp.sum(gv.astype(f32), 0))
        g_qkv = jnp.concatenate([gq, gk, gv], axis=1)
        g_tokens = g_tokens + dot(g_qkv, a_blocks[s][:, : 3 * part], (1, 1))
        g_mixed.append(jnp.concatenate([dot(tokens, g_qkv, (0, 0)), g_out], axis=1))
    piece_a = links.reduce(g_mixed)

    pieces = jnp.concatenate([piece_a, piece_u, piece_d]).astype(bf16)
    step = width // CUBE
    whole = links.ordered(links.spread(pieces)).reshape(CUBE, 3, step, width)
    whole = whole.transpose(1, 0, 2, 3).reshape(3, width, width).astype(f32)
    g_a, g_u, g_d = whole[0], whole[1], whole[2]

    shared = jnp.stack([g_gain1, g_bias1, g_b_out, g_gain2, g_bias2, g_b_down])
    shared = lax.psum(shared, ("dp", "mp"))
    split = [jnp.concatenate([g_bq[s], g_bv[s], g_b_up[s]]) for s in slots]
    mine = split[0] + sum(links.shift(split[s], -s) for s in range(1, mp))
    mine = lax.psum(mine, "dp")
    return (
        out_tokens.astype(bf16),
        g_tokens.astype(bf16),
        g_a[:, :part],
        mine[:part],
        g_a[:, part : 2 * part],
        g_a[:, 2 * part : 3 * part],
        mine[part : 2 * part],
        g_a[:, 3 * part :].T,
        shared[2],
        shared[0],
        shared[1],
        g_u,
        mine[2 * part :],
        g_d,
        shared[5],
        shared[3],
        shared[4],
    )


def solution(mesh):
    rows, cols = P(("dp", "mp"), None), P(None, "mp")
    in_specs = (
        rows,
        P("dp", None),
        cols,
        P("mp"),
        cols,
        cols,
        P("mp"),
        P("mp", None),
        P(),
        P(),
        P(),
        cols,
        P("mp"),
        P("mp", None),
        P(),
        P(),
        P(),
        rows,
    )
    out_specs = (
        rows,
        rows,
        cols,
        P("mp"),
        cols,
        cols,
        P("mp"),
        P("mp", None),
        P(),
        P(),
        P(),
        cols,
        P("mp"),
        P("mp", None),
        P(),
        P(),
        P(),
    )
    dp, mp = mesh.shape["dp"], mesh.shape["mp"]

    def step(*args):
        return per_device(dp, mp, *args)

    return jax.shard_map(step, mesh=mesh, in_specs=in_specs, out_specs=out_specs, check_vma=False)
```

time: 945 us -> 422 us (0.45)
  waiting for transfers between devices: 680 us -> 102 us
  starting transfers between devices: 1.01 us -> 87.6 us
  matrix products: 106 us -> 74.6 us
  local copies, waits for them, and re-layouts: 40.7 us -> 53.9 us
  between operations: 14.7 us -> 3.57 us
    reduce_scatter x4 -> x0, waiting for transfers between devices: 324 us -> none  [the longest x1 110 us: per_device(): lax.psum_scatter(hidden_terms(g_pre, w_up), 'mp', scatter_dimension=0, ti...]
    all_gather x4 -> x0, waiting for transfers between devices: 257 us -> none  [the longest x1 66.5 us: per_device(): full_tokens = lax.all_gather(tokens, 'mp', axis=0, tiled=True)]
    ppermute x0 -> x71, waiting for transfers between devices: none -> 102 us  [the longest x47 76.7 us: flip(): return lax.ppermute(x, 'dp', [(i, i ^ bit) for i in range(self.dp)])]
    psum x1 -> x0, waiting for transfers between devices: 98.3 us -> none  [per_device(): lax.psum((grad_w_query, grad_b_query, grad_w_key, grad_w_value, grad_b_va...]
    ppermute x0 -> x71, starting transfers between devices: none -> 87.6 us  [the longest x24 47.5 us: shift(): lax.ppermute(x, 'mp', [(i, (i + by) % self.mp) for i in range(self.mp)])]
    dot_general x42 -> x68, matrix products: 99.4 us -> 71.8 us  [the longest x48 48.7 us: dot(): lax.dot_general(left, right, ((dims[:1], dims[1:]), ((), ())), preferred_...]
    concatenate x0 -> x17, local copies, waits for them, and re-layouts: none -> 14.4 us  [the longest x4 8.7 us: per_device(): g_mixed.append(jnp.concatenate([dot(tokens, g_qkv, (0, 0)), g_out], axis=1))]
    unnamed x90 -> x229, local copies, waits for them, and re-layouts: 18.7 us -> 27.9 us
  transfers between devices with their start and end apart: 9 -> 71, of which waited for: 8 -> 36; matrix products, arithmetic and copies ran while one was open for 3% -> 19% of each run, Pallas kernels for 0% -> 0%
where the time goes in v1:
time: 422 us; the launch traced here: 417 us
  waiting for transfers between devices  102 us (24%)
  starting transfers between devices  87.6 us (21%)
  matrix products  74.6 us (18%)
  blocking collectives  58.8 us (14%)
  local copies, waits for them, and re-layouts  53.9 us (13%)
  other arithmetic  35.9 us (9%)
    ppermute x47, waiting for transfers between devices, flip(): return lax.ppermute(x, 'dp', [(i, i ^ bit) for i in range(self.dp)])  76.7 us
    dot_general x48, matrix products, dot(): lax.dot_general(left, right, ((dims[:1], dims[1:]), ((), ())), preferred_...  48.7 us
    ppermute x24, starting transfers between devices, shift(): lax.ppermute(x, 'mp', [(i, (i + by) % self.mp) for i in range(self.mp)])  47.5 us
    psum x1, blocking collectives, per_device(): shared = lax.psum(shared, ('dp', 'mp'))  40.9 us
    ppermute x47, starting transfers between devices, flip(): return lax.ppermute(x, 'dp', [(i, i ^ bit) for i in range(self.dp)])  40.1 us
    unnamed x229, local copies, waits for them, and re-layouts  27.9 us
    ppermute x24, waiting for transfers between devices, shift(): lax.ppermute(x, 'mp', [(i, (i + by) % self.mp) for i in range(self.mp)])  25.7 us
    psum x1, blocking collectives, per_device(): mine = lax.psum(mine, 'dp')  17.9 us
  transfers between devices with their start and end apart: 71, of which 36 were waited for; matrix products, arithmetic and copies ran while one was open for 19% of the time, Pallas kernels for 0%

profile of v1, /device:TPU:0, one launch (start us, length us, event | category | flops | bytes accessed | tf_op | source)
XLA Modules:
  0.0 416.8 jit_solution(2598088407525156642)
XLA Ops:
  2.4 3.0 collective-permute-start.25
  5.5 2.6 collective-permute-start.26
  9.4 2.1 concatenate.93
  31.6 3.6 collective-permute-done.11
  39.1 3.0 collective-permute-start.15
  44.2 3.3 collective-permute-done.14
  51.8 4.2 %collective-permute-done.15 = bf16[96,768]{1,0:T(8,128)(2,1)S(1)} collective-permute-done((bf16[96,768]{1,0:T(8,128)(2,1)S(1)}, bf16[96,768]{1,0:T(8,128)(2,1)S(1)}, u32[]{:S(2)}, u32[]{:S(2)}) %collective-permute-start.15) | collective-permute-done | bytes 147488 | tf_op jit(solution)/shard_map/ppermute | solution.py:51
  59.2 2.6 collective-permute-done.29
  63.4 6.3 %collective-permute-done.4 = bf16[288,768]{1,0:T(8,128)(2,1)S(1)} collective-permute-done((bf16[288,768]{1,0:T(8,128)(2,1)S(1)}, bf16[288,768]{1,0:T(8,128)(2,1)S(1)}, u32[]{:S(2)}, u32[]{:S(2)}) %collective-permute-start.4) | collective-permute-done | bytes 442400 | tf_op jit(solution)/shard_map/ppermute | solution.py:54
  75.7 7.0 %collective-permute-done.18 = bf16[288,768]{1,0:T(8,128)(2,1)S(1)} collective-permute-done((bf16[288,768]{1,0:T(8,128)(2,1)S(1)}, bf16[288,768]{1,0:T(8,128)(2,1)S(1)}, u32[]{:S(2)}, u32[]{:S(2)}) %collective-permute-start.18) | collective-permute-done | bytes 442400 | tf_op jit(solution)/shard_map/ppermute | solution.py:54
  85.9 3.2 collective-permute-done.33
  89.6 3.8 collective-permute-done.8
  93.4 2.3 collective-permute-done.22
  116.2 2.0 multiply_convert_fusion.7
  126.8 2.1 fusion.177
  133.2 2.1 convert_reduce_fusion.3
  183.6 2.0 copy-done.7
  193.9 2.4 copy.90
  199.2 2.4 copy.89
  204.5 2.4 copy.88
  206.8 2.3 pad_maximum_fusion
  209.3 2.0 copy-done.5
  216.0 3.2 collective-permute-start.68
  225.7 6.5 %collective-permute-start.70 = (f32[1152]{0:T(1024)S(1)}, f32[1152]{0:T(1024)S(1)}, u32[]{:S(2)}, u32[]{:S(2)}) collective-permute-start(f32[1152]{0:T(1024)S(1)} %concatenate.115), channel_id=1, source_target_pairs={{0,1},{1,2},{2,3},{3,0},{4,5},{5,6},{6,7},{7,4},{8,9},{9,10},{10,1... | collective-permute-start | bytes 13832 | tf_op jit(solution)/shard_map/ppermute | solution.py:51
  232.7 40.9 %psum.15 = f32[6,768]{1,0:T(8,128)S(1)} all-reduce(f32[6,768]{1,0:T(8,128)S(1)} %stack.372), channel_id=1, replica_groups=mesh['dp'=8,'mp'=4] {'dp','mp'}, use_global_device_ids=true, to_apply=%region_39.40 | all-reduce | flops 4608 | bytes 36864 | tf_op jit(solution)/shard_map/psum | solution.py:239
  274.3 5.6 %fusion.59 = (bf16[4,96,768]{2,1,0:T(8,128)(2,1)S(1)}, bf16[4,96,768]{2,1,0:T(8,128)(2,1)S(1)}, bf16[4,96,768]{2,1,0:T(8,128)(2,1)S(1)}, bf16[4,96,768]{2,1,0:T(...) fusion(bf16[4,8,96,768]{3,2,0,1:T(8,128)(2,1)} %copy-done.6, ...), kind=kLoop, calls=%fused_computation.155 | loop fusion | flops 9437184 | bytes 14155792 | tf_op jit(solution)/shard_map/convert_element_type | solution.py:94
  280.0 2.3 collective-permute-start.53
  284.8 2.2 fusion.67
  287.4 9.3 %collective-permute-done.53 = bf16[2,2,96,768]{3,2,1,0:T(8,128)(2,1)S(1)} collective-permute-done((bf16[2,2,96,768]{3,2,1,0:T(8,128)(2,1)S(1)}, bf16[2,2,96,768]{3,2,1,0:T(8,128)(2,1)S(1)}, u32[]{:S(2)}, u32[]{:S(2)}) %collective-permute-start.53) | collective-permute-done | bytes 589856 | tf_op jit(solution)/shard_map/ppermute | solution.py:54
  296.6 2.0 collective-permute-start.48
  300.4 8.9 %collective-permute-done.45 = bf16[2,2,96,768]{3,2,1,0:T(8,128)(2,1)S(1)} collective-permute-done((bf16[2,2,96,768]{3,2,1,0:T(8,128)(2,1)S(1)}, bf16[2,2,96,768]{3,2,1,0:T(8,128)(2,1)S(1)}, u32[]{:S(2)}, u32[]{:S(2)}) %collective-permute-start.45) | collective-permute-done | bytes 589856 | tf_op jit(solution)/shard_map/ppermute | solution.py:54
  309.3 2.0 collective-permute-start.40
  311.6 8.7 %collective-permute-done.37 = bf16[2,2,96,768]{3,2,1,0:T(8,128)(2,1)S(1)} collective-permute-done((bf16[2,2,96,768]{3,2,1,0:T(8,128)(2,1)S(1)}, bf16[2,2,96,768]{3,2,1,0:T(8,128)(2,1)S(1)}, u32[]{:S(2)}, u32[]{:S(2)}) %collective-permute-start.37) | collective-permute-done | bytes 589856 | tf_op jit(solution)/shard_map/ppermute | solution.py:54
  322.0 3.5 collective-permute-done.40
  325.6 2.0 collective-permute-start.46
  327.7 4.2 %collective-permute-done.54 = bf16[2,96,768]{2,1,0:T(8,128)(2,1)S(1)} collective-permute-done((bf16[2,96,768]{2,1,0:T(8,128)(2,1)S(1)}, bf16[2,96,768]{2,1,0:T(8,128)(2,1)S(1)}, u32[]{:S(2)}, u32[]{:S(2)}) %collective-permute-start.54) | collective-permute-done | bytes 294944 | tf_op jit(solution)/shard_map/ppermute | solution.py:54
  331.9 2.0 collective-permute-start.49
  340.8 2.2 collective-permute-start.58
  344.4 2.3 collective-permute-start.55
  347.8 7.6 %collective-permute-done.58 = bf16[96,768]{1,0:T(8,128)(2,1)S(1)} collective-permute-done((bf16[96,768]{1,0:T(8,128)(2,1)S(1)}, bf16[96,768]{1,0:T(8,128)(2,1)S(1)}, u32[]{:S(2)}, u32[]{:S(2)}) %collective-permute-start.58) | collective-permute-done | bytes 147488 | tf_op jit(solution)/shard_map/ppermute | solution.py:51
  355.4 3.5 collective-permute-start.47
  359.0 6.5 %collective-permute-start.43 = (bf16[96,768]{1,0:T(8,128)(2,1)S(1)}, bf16[96,768]{1,0:T(8,128)(2,1)S(1)}, u32[]{:S(2)}, u32[]{:S(2)}) collective-permute-start(bf16[96,768]{1,0:T(8,128)(2,1)S(1)} %get-tuple-element.114), channel_id=1, source_target_pairs={{0,1},{1,2},{2,3},{3,0},{4,5},{5,6},{6,7},{7,4},{8,9},{9,10},{10,1... | collective-permute-start | bytes 442376 | tf_op jit(solution)/shard_map/ppermute | solution.py:51
  365.5 3.0 collective-permute-done.50
  368.7 2.9 collective-permute-start.39
  371.7 3.2 collective-permute-start.69
  379.3 17.9 %psum.14 = f32[1152]{0:T(1024)S(1)} all-reduce(f32[1152]{0:T(1024)S(1)} %add_add_fusion.3), channel_id=1, replica_groups=mesh['dp'=8,'mp'=4] {'dp'}, use_global_device_ids=true, to_apply=%region_32.33 | all-reduce | flops 1152 | bytes 9216 | tf_op jit(solution)/shard_map/psum | solution.py:242
  400.6 4.3 %collective-permute-done.65 = bf16[144,768]{1,0:T(8,128)(2,1)S(1)} collective-permute-done((bf16[144,768]{1,0:T(8,128)(2,1)S(1)}, bf16[144,768]{1,0:T(8,128)(2,1)S(1)}, u32[]{:S(2)}, u32[]{:S(2)}) %collective-permute-start.65) | collective-permute-done | bytes 221216 | tf_op jit(solution)/shard_map/ppermute | solution.py:54
  409.0 2.7 fusion.180
  (561 shorter events, 187.2 us)
Async XLA Ops:
  2.4 32.8 %collective-permute-start.25 = (bf16[96,768]{1,0:T(8,128)(2,1)}, bf16[96,768]{1,0:T(8,128)(2,1)}, u32[]{:S(2)}, u32[]{:S(2)}) collective-permute-start(bf16[96,768]{1,0:T(8,128)(2,1)} %constant_dynamic-slice_fusion), channel_id=1, source_target_pairs={{0,1},{1,2},{2,3},{3,0},{4,5},{5,6},{6,7},{7,4},{8,9},{9,10},{10,1... | collective-permute-start | bytes 442376 | tf_op jit(solution)/shard_map/ppermute | solution.py:51
  5.5 31.1 %collective-permute-start.26 = (bf16[96,768]{1,0:T(8,128)(2,1)}, bf16[96,768]{1,0:T(8,128)(2,1)}, u32[]{:S(2)}, u32[]{:S(2)}) collective-permute-start(bf16[96,768]{1,0:T(8,128)(2,1)} %constant_dynamic-slice_fusion), channel_id=1, source_target_pairs={{0,2},{1,3},{2,0},{3,1},{4,6},{5,7},{6,4},{7,5},{8,10},{9,11},{10,... | collective-permute-start | bytes 442376 | tf_op jit(solution)/shard_map/ppermute | solution.py:51
  8.1 31.1 %collective-permute-start.27 = (bf16[96,768]{1,0:T(8,128)(2,1)}, bf16[96,768]{1,0:T(8,128)(2,1)}, u32[]{:S(2)}, u32[]{:S(2)}) collective-permute-start(bf16[96,768]{1,0:T(8,128)(2,1)} %constant_dynamic-slice_fusion), channel_id=1, source_target_pairs={{0,3},{1,0},{2,1},{3,2},{4,7},{5,4},{6,5},{7,6},{8,11},{9,8},{10,9... | collective-permute-start | bytes 442376 | tf_op jit(solution)/shard_map/ppermute | solution.py:51
  11.5 18.0 %collective-permute-start.13 = (bf16[1152]{0:T(1024)(128)(2,1)S(1)}, bf16[1152]{0:T(1024)(128)(2,1)S(1)}, u32[]{:S(2)}, u32[]{:S(2)}) collective-permute-start(bf16[1152]{0:T(1024)(128)(2,1)S(1)} %concatenate.93), channel_id=1, source_target_pairs={{0,3},{1,0},{2,1},{3,2},{4,7},{5,4},{6,5},{7,6},{8,11},{9,8},{10,9... | collective-permute-start | bytes 6920 | tf_op jit(solution)/shard_map/ppermute | solution.py:51
  11.9 17.7 %collective-permute-start.12 = (bf16[1152]{0:T(1024)(128)(2,1)S(1)}, bf16[1152]{0:T(1024)(128)(2,1)S(1)}, u32[]{:S(2)}, u32[]{:S(2)}) collective-permute-start(bf16[1152]{0:T(1024)(128)(2,1)S(1)} %concatenate.93), channel_id=1, source_target_pairs={{0,2},{1,3},{2,0},{3,1},{4,6},{5,7},{6,4},{7,5},{8,10},{9,11},{10,... | collective-permute-start | bytes 6920 | tf_op jit(solution)/shard_map/ppermute | solution.py:51
  29.7 13.4 %collective-permute-start = (bf16[96,768]{1,0:T(8,128)(2,1)S(1)}, bf16[96,768]{1,0:T(8,128)(2,1)S(1)}, u32[]{:S(2)}, u32[]{:S(2)}) collective-permute-start(bf16[96,768]{1,0:T(8,128)(2,1)S(1)} %fusion.167), channel_id=1, source_target_pairs={{0,1},{1,2},{2,3},{3,0},{4,5},{5,6},{6,7},{7,4},{8,9},{9,10},{10,1... | collective-permute-start | bytes 442376 | tf_op jit(solution)/shard_map/ppermute | solution.py:51
  35.1 13.6 %collective-permute-start.1 = (bf16[96,768]{1,0:T(8,128)(2,1)S(1)}, bf16[96,768]{1,0:T(8,128)(2,1)S(1)}, u32[]{:S(2)}, u32[]{:S(2)}) collective-permute-start(bf16[96,768]{1,0:T(8,128)(2,1)S(1)} %fusion.167), channel_id=1, source_target_pairs={{0,2},{1,3},{2,0},{3,1},{4,6},{5,7},{6,4},{7,5},{8,10},{9,11},{10,... | collective-permute-start | bytes 442376 | tf_op jit(solution)/shard_map/ppermute | solution.py:51
  35.2 15.0 %collective-permute-start.2 = (bf16[96,768]{1,0:T(8,128)(2,1)S(1)}, bf16[96,768]{1,0:T(8,128)(2,1)S(1)}, u32[]{:S(2)}, u32[]{:S(2)}) collective-permute-start(bf16[96,768]{1,0:T(8,128)(2,1)S(1)} %fusion.167), channel_id=1, source_target_pairs={{0,3},{1,0},{2,1},{3,2},{4,7},{5,4},{6,5},{7,6},{8,11},{9,8},{10,9... | collective-permute-start | bytes 442376 | tf_op jit(solution)/shard_map/ppermute | solution.py:51
  36.6 10.9 %collective-permute-start.14 = (bf16[96,768]{1,0:T(8,128)(2,1)S(1)}, bf16[96,768]{1,0:T(8,128)(2,1)S(1)}, u32[]{:S(2)}, u32[]{:S(2)}) collective-permute-start(bf16[96,768]{1,0:T(8,128)(2,1)S(1)} %constant_dynamic-slice_fusion.1), channel_id=1, source_target_pairs={{0,1},{1,2},{2,3},{3,0},{4,5},{5,6},{6,7},{7,4},{8,9},{9,10},{10,1... | collective-permute-start | bytes 442376 | tf_op jit(solution)/shard_map/ppermute | solution.py:51
  39.1 16.8 %collective-permute-start.15 = (bf16[96,768]{1,0:T(8,128)(2,1)S(1)}, bf16[96,768]{1,0:T(8,128)(2,1)S(1)}, u32[]{:S(2)}, u32[]{:S(2)}) collective-permute-start(bf16[96,768]{1,0:T(8,128)(2,1)S(1)} %constant_dynamic-slice_fusion.1), channel_id=1, source_target_pairs={{0,2},{1,3},{2,0},{3,1},{4,6},{5,7},{6,4},{7,5},{8,10},{9,11},{10,... | collective-permute-start | bytes 442376 | tf_op jit(solution)/shard_map/ppermute | solution.py:51
  43.1 14.4 %collective-permute-start.16 = (bf16[96,768]{1,0:T(8,128)(2,1)S(1)}, bf16[96,768]{1,0:T(8,128)(2,1)S(1)}, u32[]{:S(2)}, u32[]{:S(2)}) collective-permute-start(bf16[96,768]{1,0:T(8,128)(2,1)S(1)} %constant_dynamic-slice_fusion.1), channel_id=1, source_target_pairs={{0,3},{1,0},{2,1},{3,2},{4,7},{5,4},{6,5},{7,6},{8,11},{9,8},{10,9... | collective-permute-start | bytes 442376 | tf_op jit(solution)/shard_map/ppermute | solution.py:51
  47.5 25.3 %collective-permute-start.28 = (bf16[288,768]{1,0:T(8,128)(2,1)S(1)}, bf16[288,768]{1,0:T(8,128)(2,1)S(1)}, u32[]{:S(2)}, u32[]{:S(2)}) collective-permute-start(bf16[288,768]{1,0:T(8,128)(2,1)S(1)} %constant_dynamic-update-slice_fusion.13), channel_id=1, source_target_pairs={{0,4},{4,0},{8,12},{12,8},{16,20},{20,16},{24,28},{28,24},{1,5},{5... | collective-permute-start | bytes 1327112 | tf_op jit(solution)/shard_map/ppermute | solution.py:54
  48.7 13.1 %collective-permute-start.29 = (bf16[288,768]{1,0:T(8,128)(2,1)S(1)}, bf16[288,768]{1,0:T(8,128)(2,1)S(1)}, u32[]{:S(2)}, u32[]{:S(2)}) collective-permute-start(bf16[288,768]{1,0:T(8,128)(2,1)S(1)} %constant_dynamic-update-slice_fusion.13), channel_id=1, source_target_pairs={{0,8},{4,12},{8,0},{12,4},{16,24},{20,28},{24,16},{28,20},{1,9},{5... | collective-permute-start | bytes 1327112 | tf_op jit(solution)/shard_map/ppermute | solution.py:54
  50.2 13.2 %collective-permute-start.31 = (bf16[288,768]{1,0:T(8,128)(2,1)S(1)}, bf16[288,768]{1,0:T(8,128)(2,1)S(1)}, u32[]{:S(2)}, u32[]{:S(2)}) collective-permute-start(bf16[288,768]{1,0:T(8,128)(2,1)S(1)} %constant_dynamic-update-slice_fusion.13), channel_id=1, source_target_pairs={{0,16},{4,20},{8,24},{12,28},{16,0},{20,4},{24,8},{28,12},{1,17},{... | collective-permute-start | bytes 1327112 | tf_op jit(solution)/shard_map/ppermute | solution.py:54
  56.0 13.7 %collective-permute-start.4 = (bf16[288,768]{1,0:T(8,128)(2,1)S(1)}, bf16[288,768]{1,0:T(8,128)(2,1)S(1)}, u32[]{:S(2)}, u32[]{:S(2)}) collective-permute-start(bf16[288,768]{1,0:T(8,128)(2,1)S(1)} %constant_dynamic-update-slice_fusion.3), channel_id=1, source_target_pairs={{0,8},{4,12},{8,0},{12,4},{16,24},{20,28},{24,16},{28,20},{1,9},{5... | collective-permute-start | bytes 1327112 | tf_op jit(solution)/shard_map/ppermute | solution.py:54
  57.5 13.7 %collective-permute-start.6 = (bf16[288,768]{1,0:T(8,128)(2,1)S(1)}, bf16[288,768]{1,0:T(8,128)(2,1)S(1)}, u32[]{:S(2)}, u32[]{:S(2)}) collective-permute-start(bf16[288,768]{1,0:T(8,128)(2,1)S(1)} %constant_dynamic-update-slice_fusion.3), channel_id=1, source_target_pairs={{0,16},{4,20},{8,24},{12,28},{16,0},{20,4},{24,8},{28,12},{1,17},{... | collective-permute-start | bytes 1327112 | tf_op jit(solution)/shard_map/ppermute | solution.py:54
  61.8 11.7 %collective-permute-start.3 = (bf16[288,768]{1,0:T(8,128)(2,1)S(1)}, bf16[288,768]{1,0:T(8,128)(2,1)S(1)}, u32[]{:S(2)}, u32[]{:S(2)}) collective-permute-start(bf16[288,768]{1,0:T(8,128)(2,1)S(1)} %constant_dynamic-update-slice_fusion.3), channel_id=1, source_target_pairs={{0,4},{4,0},{8,12},{12,8},{16,20},{20,16},{24,28},{28,24},{1,5},{5... | collective-permute-start | bytes 1327112 | tf_op jit(solution)/shard_map/ppermute | solution.py:54
  69.7 13.1 %collective-permute-start.18 = (bf16[288,768]{1,0:T(8,128)(2,1)S(1)}, bf16[288,768]{1,0:T(8,128)(2,1)S(1)}, u32[]{:S(2)}, u32[]{:S(2)}) collective-permute-start(bf16[288,768]{1,0:T(8,128)(2,1)S(1)} %constant_dynamic-update-slice_fusion.8), channel_id=1, source_target_pairs={{0,8},{4,12},{8,0},{12,4},{16,24},{20,28},{24,16},{28,20},{1,9},{5... | collective-permute-start | bytes 1327112 | tf_op jit(solution)/shard_map/ppermute | solution.py:54
  71.2 13.2 %collective-permute-start.20 = (bf16[288,768]{1,0:T(8,128)(2,1)S(1)}, bf16[288,768]{1,0:T(8,128)(2,1)S(1)}, u32[]{:S(2)}, u32[]{:S(2)}) collective-permute-start(bf16[288,768]{1,0:T(8,128)(2,1)S(1)} %constant_dynamic-update-slice_fusion.8), channel_id=1, source_target_pairs={{0,16},{4,20},{8,24},{12,28},{16,0},{20,4},{24,8},{28,12},{1,17},{... | collective-permute-start | bytes 1327112 | tf_op jit(solution)/shard_map/ppermute | solution.py:54
  72.8 16.3 %collective-permute-start.33 = (bf16[144,768]{1,0:T(8,128)(2,1)S(1)}, bf16[144,768]{1,0:T(8,128)(2,1)S(1)}, u32[]{:S(2)}, u32[]{:S(2)}) collective-permute-start(bf16[144,768]{1,0:T(8,128)(2,1)S(1)} %slice.538), channel_id=1, source_target_pairs={{0,16},{4,20},{8,24},{12,28},{16,0},{20,4},{24,8},{28,12},{1,17},{... | collective-permute-start | bytes 663560 | tf_op jit(solution)/shard_map/ppermute | solution.py:54
  73.4 22.4 %collective-permute-start.34 = (bf16[144,768]{1,0:T(8,128)(2,1)S(1)}, bf16[144,768]{1,0:T(8,128)(2,1)S(1)}, u32[]{:S(2)}, u32[]{:S(2)}) collective-permute-start(bf16[144,768]{1,0:T(8,128)(2,1)S(1)} %slice.539), channel_id=1, source_target_pairs={{0,8},{4,12},{8,0},{12,4},{16,24},{20,28},{24,16},{28,20},{1,9},{5... | collective-permute-start | bytes 663560 | tf_op jit(solution)/shard_map/ppermute | solution.py:54
  74.1 19.3 %collective-permute-start.8 = (bf16[144,768]{1,0:T(8,128)(2,1)S(1)}, bf16[144,768]{1,0:T(8,128)(2,1)S(1)}, u32[]{:S(2)}, u32[]{:S(2)}) collective-permute-start(bf16[144,768]{1,0:T(8,128)(2,1)S(1)} %slice.508), channel_id=1, source_target_pairs={{0,16},{4,20},{8,24},{12,28},{16,0},{20,4},{24,8},{28,12},{1,17},{... | collective-permute-start | bytes 663560 | tf_op jit(solution)/shard_map/ppermute | solution.py:54
  82.8 13.6 %collective-permute-start.9 = (bf16[144,768]{1,0:T(8,128)(2,1)S(1)}, bf16[144,768]{1,0:T(8,128)(2,1)S(1)}, u32[]{:S(2)}, u32[]{:S(2)}) collective-permute-start(bf16[144,768]{1,0:T(8,128)(2,1)S(1)} %slice.509), channel_id=1, source_target_pairs={{0,8},{4,12},{8,0},{12,4},{16,24},{20,28},{24,16},{28,20},{1,9},{5... | collective-permute-start | bytes 663560 | tf_op jit(solution)/shard_map/ppermute | solution.py:54
  84.3 11.4 %collective-permute-start.22 = (bf16[144,768]{1,0:T(8,128)(2,1)S(1)}, bf16[144,768]{1,0:T(8,128)(2,1)S(1)}, u32[]{:S(2)}, u32[]{:S(2)}) collective-permute-start(bf16[144,768]{1,0:T(8,128)(2,1)S(1)} %slice.534), channel_id=1, source_target_pairs={{0,16},{4,20},{8,24},{12,28},{16,0},{20,4},{24,8},{28,12},{1,17},{... | collective-permute-start | bytes 663560 | tf_op jit(solution)/shard_map/ppermute | solution.py:54
  98.8 15.6 %collective-permute-start.24 = (bf16[288,768]{1,0:T(8,128)(2,1)S(1)}, bf16[288,768]{1,0:T(8,128)(2,1)S(1)}, u32[]{:S(2)}, u32[]{:S(2)}) collective-permute-start(bf16[288,768]{1,0:T(8,128)(2,1)S(1)} %constant_dynamic-update-slice_fusion.11), channel_id=1, source_target_pairs={{0,4},{4,0},{8,12},{12,8},{16,20},{20,16},{24,28},{28,24},{1,5},{5... | collective-permute-start | bytes 1327112 | tf_op jit(solution)/shard_map/ppermute | solution.py:54
  182.7 91.6 %collective-permute-start.52 = (bf16[4,4,96,768]{3,2,1,0:T(8,128)(2,1)}, bf16[4,4,96,768]{3,2,1,0:T(8,128)(2,1)}, u32[]{:S(2)}, u32[]{:S(2)}) collective-permute-start(bf16[4,4,96,768]{3,2,1,0:T(8,128)(2,1)} %pad_maximum_fusion.9), channel_id=1, source_target_pairs={{0,4},{4,0},{8,12},{12,8},{16,20},{20,16},{24,28},{28,24},{1,5},{5... | collective-permute-start | bytes 7077896 | tf_op jit(solution)/shard_map/ppermute | solution.py:54
  187.3 87.0 %collective-permute-start.44 = (bf16[4,4,96,768]{3,2,1,0:T(8,128)(2,1)}, bf16[4,4,96,768]{3,2,1,0:T(8,128)(2,1)}, u32[]{:S(2)}, u32[]{:S(2)}) collective-permute-start(bf16[4,4,96,768]{3,2,1,0:T(8,128)(2,1)} %pad_maximum_fusion.8), channel_id=1, source_target_pairs={{0,4},{4,0},{8,12},{12,8},{16,20},{20,16},{24,28},{28,24},{1,5},{5... | collective-permute-start | bytes 7077896 | tf_op jit(solution)/shard_map/ppermute | solution.py:54
  213.0 71.2 %collective-permute-start.36 = (bf16[4,4,96,768]{3,2,1,0:T(8,128)(2,1)}, bf16[4,4,96,768]{3,2,1,0:T(8,128)(2,1)}, u32[]{:S(2)}, u32[]{:S(2)}) collective-permute-start(bf16[4,4,96,768]{3,2,1,0:T(8,128)(2,1)} %pad_maximum_fusion.7), channel_id=1, source_target_pairs={{0,4},{4,0},{8,12},{12,8},{16,20},{20,16},{24,28},{28,24},{1,5},{5... | collective-permute-start | bytes 7077896 | tf_op jit(solution)/shard_map/ppermute | solution.py:54
  216.0 162.6 %collective-permute-start.68 = (f32[1152]{0:T(1024)}, f32[1152]{0:T(1024)}, u32[]{:S(2)}, u32[]{:S(2)}) collective-permute-start(f32[1152]{0:T(1024)} %concatenate.113), channel_id=1, source_target_pairs={{0,3},{1,0},{2,1},{3,2},{4,7},{5,4},{6,5},{7,6},{8,11},{9,8},{10,9... | collective-permute-start | bytes 13832 | tf_op jit(solution)/shard_map/ppermute | solution.py:51
  225.7 151.3 %collective-permute-start.70 = (f32[1152]{0:T(1024)S(1)}, f32[1152]{0:T(1024)S(1)}, u32[]{:S(2)}, u32[]{:S(2)}) collective-permute-start(f32[1152]{0:T(1024)S(1)} %concatenate.115), channel_id=1, source_target_pairs={{0,1},{1,2},{2,3},{3,0},{4,5},{5,6},{6,7},{7,4},{8,9},{9,10},{10,1... | collective-permute-start | bytes 13832 | tf_op jit(solution)/shard_map/ppermute | solution.py:51
  280.0 16.6 %collective-permute-start.53 = (bf16[2,2,96,768]{3,2,1,0:T(8,128)(2,1)S(1)}, bf16[2,2,96,768]{3,2,1,0:T(8,128)(2,1)S(1)}, u32[]{:S(2)}, u32[]{:S(2)}) collective-permute-start(bf16[2,2,96,768]{3,2,1,0:T(8,128)(2,1)S(1)} %pad_maximum_fusion.18), channel_id=1, source_target_pairs={{0,8},{4,12},{8,0},{12,4},{16,24},{20,28},{24,16},{28,20},{1,9},{5... | collective-permute-start | bytes 1769480 | tf_op jit(solution)/shard_map/ppermute | solution.py:54
  282.5 16.3 %collective-permute-start.56 = (bf16[2,2,96,768]{3,2,1,0:T(8,128)(2,1)S(1)}, bf16[2,2,96,768]{3,2,1,0:T(8,128)(2,1)S(1)}, u32[]{:S(2)}, u32[]{:S(2)}) collective-permute-start(bf16[2,2,96,768]{3,2,1,0:T(8,128)(2,1)S(1)} %pad_maximum_fusion.19), channel_id=1, source_target_pairs={{0,16},{4,20},{8,24},{12,28},{16,0},{20,4},{24,8},{28,12},{1,17},{... | collective-permute-start | bytes 1769480 | tf_op jit(solution)/shard_map/ppermute | solution.py:54
  284.2 25.0 %collective-permute-start.45 = (bf16[2,2,96,768]{3,2,1,0:T(8,128)(2,1)S(1)}, bf16[2,2,96,768]{3,2,1,0:T(8,128)(2,1)S(1)}, u32[]{:S(2)}, u32[]{:S(2)}) collective-permute-start(bf16[2,2,96,768]{3,2,1,0:T(8,128)(2,1)S(1)} %pad_maximum_fusion.16), channel_id=1, source_target_pairs={{0,8},{4,12},{8,0},{12,4},{16,24},{20,28},{24,16},{28,20},{1,9},{5... | collective-permute-start | bytes 1769480 | tf_op jit(solution)/shard_map/ppermute | solution.py:54
  296.6 14.8 %collective-permute-start.48 = (bf16[2,2,96,768]{3,2,1,0:T(8,128)(2,1)S(1)}, bf16[2,2,96,768]{3,2,1,0:T(8,128)(2,1)S(1)}, u32[]{:S(2)}, u32[]{:S(2)}) collective-permute-start(bf16[2,2,96,768]{3,2,1,0:T(8,128)(2,1)S(1)} %pad_maximum_fusion.17), channel_id=1, source_target_pairs={{0,16},{4,20},{8,24},{12,28},{16,0},{20,4},{24,8},{28,12},{1,17},{... | collective-permute-start | bytes 1769480 | tf_op jit(solution)/shard_map/ppermute | solution.py:54
  298.8 21.5 %collective-permute-start.37 = (bf16[2,2,96,768]{3,2,1,0:T(8,128)(2,1)S(1)}, bf16[2,2,96,768]{3,2,1,0:T(8,128)(2,1)S(1)}, u32[]{:S(2)}, u32[]{:S(2)}) collective-permute-start(bf16[2,2,96,768]{3,2,1,0:T(8,128)(2,1)S(1)} %pad_maximum_fusion.14), channel_id=1, source_target_pairs={{0,8},{4,12},{8,0},{12,4},{16,24},{20,28},{24,16},{28,20},{1,9},{5... | collective-permute-start | bytes 1769480 | tf_op jit(solution)/shard_map/ppermute | solution.py:54
  309.3 16.3 %collective-permute-start.40 = (bf16[2,2,96,768]{3,2,1,0:T(8,128)(2,1)S(1)}, bf16[2,2,96,768]{3,2,1,0:T(8,128)(2,1)S(1)}, u32[]{:S(2)}, u32[]{:S(2)}) collective-permute-start(bf16[2,2,96,768]{3,2,1,0:T(8,128)(2,1)S(1)} %pad_maximum_fusion.15), channel_id=1, source_target_pairs={{0,16},{4,20},{8,24},{12,28},{16,0},{20,4},{24,8},{28,12},{1,17},{... | collective-permute-start | bytes 1769480 | tf_op jit(solution)/shard_map/ppermute | solution.py:54
  311.4 20.5 %collective-permute-start.54 = (bf16[2,96,768]{2,1,0:T(8,128)(2,1)S(1)}, bf16[2,96,768]{2,1,0:T(8,128)(2,1)S(1)}, u32[]{:S(2)}, u32[]{:S(2)}) collective-permute-start(bf16[2,96,768]{2,1,0:T(8,128)(2,1)S(1)} %fusion.127), channel_id=1, source_target_pairs={{0,16},{4,20},{8,24},{12,28},{16,0},{20,4},{24,8},{28,12},{1,17},{... | collective-permute-start | bytes 884744 | tf_op jit(solution)/shard_map/ppermute | solution.py:54
  320.2 13.7 %collective-permute-start.57 = (bf16[2,96,768]{2,1,0:T(8,128)(2,1)S(1)}, bf16[2,96,768]{2,1,0:T(8,128)(2,1)S(1)}, u32[]{:S(2)}, u32[]{:S(2)}) collective-permute-start(bf16[2,96,768]{2,1,0:T(8,128)(2,1)S(1)} %fusion.126), channel_id=1, source_target_pairs={{0,8},{4,12},{8,0},{12,4},{16,24},{20,28},{24,16},{28,20},{1,9},{5... | collective-permute-start | bytes 884744 | tf_op jit(solution)/shard_map/ppermute | solution.py:54
  325.6 12.1 %collective-permute-start.46 = (bf16[2,96,768]{2,1,0:T(8,128)(2,1)S(1)}, bf16[2,96,768]{2,1,0:T(8,128)(2,1)S(1)}, u32[]{:S(2)}, u32[]{:S(2)}) collective-permute-start(bf16[2,96,768]{2,1,0:T(8,128)(2,1)S(1)} %fusion.132), channel_id=1, source_target_pairs={{0,16},{4,20},{8,24},{12,28},{16,0},{20,4},{24,8},{28,12},{1,17},{... | collective-permute-start | bytes 884744 | tf_op jit(solution)/shard_map/ppermute | solution.py:54
  340.8 14.6 %collective-permute-start.58 = (bf16[96,768]{1,0:T(8,128)(2,1)S(1)}, bf16[96,768]{1,0:T(8,128)(2,1)S(1)}, u32[]{:S(2)}, u32[]{:S(2)}) collective-permute-start(bf16[96,768]{1,0:T(8,128)(2,1)S(1)} %get-tuple-element.117), channel_id=1, source_target_pairs={{0,2},{1,3},{2,0},{3,1},{4,6},{5,7},{6,4},{7,5},{8,10},{9,11},{10,... | collective-permute-start | bytes 442376 | tf_op jit(solution)/shard_map/ppermute | solution.py:51
  344.4 11.1 %collective-permute-start.55 = (bf16[96,768]{1,0:T(8,128)(2,1)S(1)}, bf16[96,768]{1,0:T(8,128)(2,1)S(1)}, u32[]{:S(2)}, u32[]{:S(2)}) collective-permute-start(bf16[96,768]{1,0:T(8,128)(2,1)S(1)} %slice_bitcast_fusion.39), channel_id=1, source_target_pairs={{0,3},{1,0},{2,1},{3,2},{4,7},{5,4},{6,5},{7,6},{8,11},{9,8},{10,9... | collective-permute-start | bytes 442376 | tf_op jit(solution)/shard_map/ppermute | solution.py:51
  347.8 11.2 %collective-permute-start.51 = (bf16[96,768]{1,0:T(8,128)(2,1)S(1)}, bf16[96,768]{1,0:T(8,128)(2,1)S(1)}, u32[]{:S(2)}, u32[]{:S(2)}) collective-permute-start(bf16[96,768]{1,0:T(8,128)(2,1)S(1)} %get-tuple-element.116), channel_id=1, source_target_pairs={{0,1},{1,2},{2,3},{3,0},{4,5},{5,6},{6,7},{7,4},{8,9},{9,10},{10,1... | collective-permute-start | bytes 442376 | tf_op jit(solution)/shard_map/ppermute | solution.py:51
  355.4 13.1 %collective-permute-start.50 = (bf16[96,768]{1,0:T(8,128)(2,1)S(1)}, bf16[96,768]{1,0:T(8,128)(2,1)S(1)}, u32[]{:S(2)}, u32[]{:S(2)}) collective-permute-start(bf16[96,768]{1,0:T(8,128)(2,1)S(1)} %get-tuple-element.115), channel_id=1, source_target_pairs={{0,2},{1,3},{2,0},{3,1},{4,6},{5,7},{6,4},{7,5},{8,10},{9,11},{10,... | collective-permute-start | bytes 442376 | tf_op jit(solution)/shard_map/ppermute | solution.py:51
  355.4 13.3 %collective-permute-start.47 = (bf16[96,768]{1,0:T(8,128)(2,1)S(1)}, bf16[96,768]{1,0:T(8,128)(2,1)S(1)}, u32[]{:S(2)}, u32[]{:S(2)}) collective-permute-start(bf16[96,768]{1,0:T(8,128)(2,1)S(1)} %slice_bitcast_fusion.43), channel_id=1, source_target_pairs={{0,3},{1,0},{2,1},{3,2},{4,7},{5,4},{6,5},{7,6},{8,11},{9,8},{10,9... | collective-permute-start | bytes 442376 | tf_op jit(solution)/shard_map/ppermute | solution.py:51
  359.0 12.7 %collective-permute-start.43 = (bf16[96,768]{1,0:T(8,128)(2,1)S(1)}, bf16[96,768]{1,0:T(8,128)(2,1)S(1)}, u32[]{:S(2)}, u32[]{:S(2)}) collective-permute-start(bf16[96,768]{1,0:T(8,128)(2,1)S(1)} %get-tuple-element.114), channel_id=1, source_target_pairs={{0,1},{1,2},{2,3},{3,0},{4,5},{5,6},{6,7},{7,4},{8,9},{9,10},{10,1... | collective-permute-start | bytes 442376 | tf_op jit(solution)/shard_map/ppermute | solution.py:51
  376.9 23.6 %collective-permute-start.60 = (bf16[288,768]{1,0:T(8,128)(2,1)S(1)}, bf16[288,768]{1,0:T(8,128)(2,1)S(1)}, u32[]{:S(2)}, u32[]{:S(2)}) collective-permute-start(bf16[288,768]{1,0:T(8,128)(2,1)S(1)} %pad_maximum_fusion.20), channel_id=1, source_target_pairs={{0,4},{4,0},{8,12},{12,8},{16,20},{20,16},{24,28},{28,24},{1,5},{5... | collective-permute-start | bytes 1327112 | tf_op jit(solution)/shard_map/ppermute | solution.py:54
  377.0 21.5 %collective-permute-start.61 = (bf16[288,768]{1,0:T(8,128)(2,1)S(1)}, bf16[288,768]{1,0:T(8,128)(2,1)S(1)}, u32[]{:S(2)}, u32[]{:S(2)}) collective-permute-start(bf16[288,768]{1,0:T(8,128)(2,1)S(1)} %pad_maximum_fusion.20), channel_id=1, source_target_pairs={{0,8},{4,12},{8,0},{12,4},{16,24},{20,28},{24,16},{28,20},{1,9},{5... | collective-permute-start | bytes 1327112 | tf_op jit(solution)/shard_map/ppermute | solution.py:54
  377.1 22.7 %collective-permute-start.63 = (bf16[288,768]{1,0:T(8,128)(2,1)S(1)}, bf16[288,768]{1,0:T(8,128)(2,1)S(1)}, u32[]{:S(2)}, u32[]{:S(2)}) collective-permute-start(bf16[288,768]{1,0:T(8,128)(2,1)S(1)} %pad_maximum_fusion.20), channel_id=1, source_target_pairs={{0,16},{4,20},{8,24},{12,28},{16,0},{20,4},{24,8},{28,12},{1,17},{... | collective-permute-start | bytes 1327112 | tf_op jit(solution)/shard_map/ppermute | solution.py:54
  (100 other events, 707.1 us)

commit v2 on v1

v2 whole, which is shorter than its diff:
```python
import functools

import jax
import jax.numpy as jnp
from jax import lax
from jax.experimental import pallas as pl
from jax.experimental.pallas import tpu as pltpu
from jax.sharding import PartitionSpec as P

HEAD_DIM = 64
EPS = 1e-05
INV_ROOT_TWO = 0.7071067811865476
INV_ROOT_TWO_PI = 0.3989422804014327
SCALE = HEAD_DIM**-0.5
CUBE = 8
TAIL = 16
EXTRA = 8

f32 = jnp.float32
bf16 = jnp.bfloat16
SDS = jax.ShapeDtypeStruct


def dot(left, right, dims):
    return lax.dot_general(left, right, ((dims[:1], dims[1:]), ((), ())), preferred_element_type=f32)


def any_spec():
    return pl.BlockSpec(memory_space=pl.ANY)


def smem_spec():
    return pl.BlockSpec(memory_space=pltpu.SMEM)


def whole(shape):
    zeros = (0,) * len(shape)
    return pl.BlockSpec(shape, lambda *_: zeros)


def cost(flops, nbytes, trans=0):
    return pl.CostEstimate(flops=int(flops), bytes_accessed=int(nbytes), transcendentals=int(trans))


def spread_copies(place, parts, rows, step, slots, put):
    half = rows // 16 * 8
    copies = []
    for j in range(2):
        piece, over_x, over_y, diag_a, diag_b = parts[5 * j : 5 * j + 5]
        for i, ref in enumerate((piece, over_x, over_y)):
            for s in range(slots):
                copies.append((ref.at[pl.ds(s * step, step)], put(2 * i + j, s, 0, step)))
        for ref, first, end in ((diag_a, 0, half), (diag_b, half, rows)):
            for s in range(slots):
                low, high = max(first, s * step), min(end, (s + 1) * step)
                if low < high:
                    copies.append((ref.at[pl.ds(low - first, high - low)], put(6 + j, s, low - s * step, high - low)))
    return copies


def run_copies(copies, sems):
    started = [pltpu.make_async_copy(a, b, sems.at[n]) for n, (a, b) in enumerate(copies)]
    for c in started:
        c.start()
    for c in started:
        c.wait()


def assemble_kernel(step, slots, place_ref, own, *refs):
    parts, out, sems = refs[:10], refs[10], refs[11]

    def put(rel, s, first, count):
        to = pl.multiple_of((place_ref[0] ^ rel) * step + first, 16)
        return out.at[s + 1, pl.ds(to, count)]

    run_copies([(own, out.at[0])] + spread_copies(place_ref[0], parts, step * slots, step, slots, put), sems)


def assemble(place, own, parts, slots):
    rows, cols = own.shape
    return pl.pallas_call(
        functools.partial(assemble_kernel, rows // CUBE, slots),
        out_shape=SDS((slots + 1, rows, cols), bf16),
        grid=(1,),
        in_specs=[smem_spec()] + [any_spec()] * 11,
        out_specs=whole((slots + 1, rows, cols)),
        scratch_shapes=[pltpu.SemaphoreType.DMA((1 + 10 * slots,))],
        cost_estimate=cost(0, 4 * (slots + 1) * rows * cols),
        name="assemble",
    )(place, own, *parts)


def block_mask(seg_ref, bias):
    rows = bias.shape[0]
    segment = jnp.broadcast_to(seg_ref[...].astype(f32), (8, rows))
    bias[...] = jnp.where(segment.T[:, 0:1] == segment[0:1], 0.0, -1e30)


def attend_kernel(part, x_ref, a_ref, tail_ref, seg_ref, qkv_out, ctx_out, lse_out, att_out, bias):
    i = pl.program_id(0)
    heads = part // HEAD_DIM

    @pl.when(i == 0)
    def _():
        block_mask(seg_ref, bias)
        att_out[...] = jnp.zeros_like(att_out)

    shift = tail_ref[0].astype(f32).T
    qkv_out[0] = (dot(a_ref[0, : 3 * part, :], x_ref[...], (1, 1)) + shift[: 3 * part, 0:1]).astype(bf16)
    sums = []
    for h in range(heads):
        here = slice(h * HEAD_DIM, (h + 1) * HEAD_DIM)
        q, k, v = [qkv_out[0, n * part + h * HEAD_DIM : n * part + (h + 1) * HEAD_DIM, :] for n in range(3)]
        scores = dot(k, q, (0, 0)) * SCALE + bias[...]
        highest = jnp.max(scores, 0, keepdims=True)
        expd = jnp.exp(scores - highest)
        total = jnp.sum(expd, 0, keepdims=True)
        probs = (expd * (1.0 / total)).astype(bf16)
        ctx_out[0, here, :] = dot(v, probs, (1, 0)).astype(bf16)
        sums.append(highest + jnp.log(total))
    lse_out[0] = jnp.concatenate(sums + [jnp.zeros_like(sums[0])] * (8 - heads), axis=0)
    att_out[...] += dot(ctx_out[0], a_ref[0, 3 * part :, :], (0, 0))


def attend(first, count, part, x, a, tails, segment):
    rows, width = x.shape
    return pl.pallas_call(
        functools.partial(attend_kernel, part),
        out_shape=(
            SDS((count, 3 * part, rows), bf16),
            SDS((count, part, rows), bf16),
            SDS((count, 8, rows), f32),
            SDS((rows, width), f32),
        ),
        grid=(count,),
        in_specs=[
            whole((rows, width)),
            pl.BlockSpec((1, width, width), lambda i: (i + first, 0, 0)),
            pl.BlockSpec((1, TAIL, width), lambda i: (i + first, 0, 0)),
            whole((1, rows)),
        ],
        out_specs=(
            pl.BlockSpec((1, 3 * part, rows), lambda i: (i, 0, 0)),
            pl.BlockSpec((1, part, rows), lambda i: (i, 0, 0)),
            pl.BlockSpec((1, 8, rows), lambda i: (i, 0, 0)),
            whole((rows, width)),
        ),
        scratch_shapes=[pltpu.VMEM((rows, rows), f32)],
        cost_estimate=cost(
            count * (2 * rows * width * width + 4 * rows * rows * part), count * 4e6, count * 3 * rows * rows
        ),
        name="attend",
    )(x, a, tails, segment)


def store_pieces(acc, place, keep, send, vec=None):
    step = acc.shape[0] // CUBE
    half = step // 2
    for c, (px, py, ra, rb) in ((0, keep), (1, send)):
        for r, (to_a, at_a, to_b, at_b) in enumerate(
            ((ra, 1, rb, 1), (px, 1, rb, 0), (ra, 0, py, 1), (px, 0, py, 0))
        ):
            owner = place ^ (2 * r + c)
            base = pl.multiple_of(owner * step, 32)
            to_b[at_b, 0] = acc[pl.ds(base, half)].astype(bf16)
            to_a[at_a, 0, 0:half] = acc[pl.ds(pl.multiple_of(base + half, 16), half)].astype(bf16)
            if vec is not None:
                row = vec[pl.ds(owner, 1)]
                to_a[at_a, 0, half:] = jnp.broadcast_to(row, (EXTRA, row.shape[1])).astype(bf16)


def piece_shapes(count, step, cols, extra):
    half = step // 2
    a, b = SDS((2, count, half + extra, cols), bf16), SDS((2, count, half, cols), bf16)
    return (a, b, a, b) * 2


def piece_specs(step, cols, extra):
    half = step // 2
    a = pl.BlockSpec((2, 1, half + extra, cols), lambda i: (0, i, 0, 0))
    b = pl.BlockSpec((2, 1, half, cols), lambda i: (0, i, 0, 0))
    return (a, b, a, b) * 2


def attend_back_kernel(
    part, last, place_ref, x_ref, ga_ref, a_ref, qkv_ref, ctx_ref, lse_ref, vec_ref, seg_ref, gtok_ref, *refs
):
    pieces, gtok_out = refs[:8], refs[8]
    bias, gc_t, g_t, acc, vec = refs[9:]
    heads = part // HEAD_DIM

    @pl.when(pl.program_id(0) == 0)
    def _():
        block_mask(seg_ref, bias)
        if not last:
            gtok_out[...] = gtok_ref[...]

    gc_t[...] = dot(a_ref[0, 3 * part :, :], ga_ref[...], (1, 1)).astype(bf16)
    for h in range(heads):
        here = [slice(n * part + h * HEAD_DIM, n * part + (h + 1) * HEAD_DIM) for n in range(3)]
        q, k, v = [qkv_ref[0, at, :] for at in here]
        g_context = gc_t[here[0], :]
        probs = jnp.exp(dot(k, q, (0, 0)) * SCALE + bias[...] - lse_ref[0, h : h + 1, :])
        g_t[here[2], :] = dot(g_context, probs.astype(bf16), (1, 1)).astype(bf16)
        g_probs = dot(v, g_context, (0, 0))
        centre = jnp.sum(probs * g_probs, 0, keepdims=True)
        g_scores = (probs * (g_probs - centre)).astype(bf16)
        g_t[here[0], :] = (dot(k, g_scores, (1, 0)) * SCALE).astype(bf16)
        g_t[here[1], :] = (dot(q, g_scores, (1, 1)) * SCALE).astype(bf16)
    acc[: 3 * part, :] = dot(g_t[...], x_ref[...], (1, 0))
    acc[3 * part :, :] = dot(ctx_ref[0], ga_ref[...], (1, 0))
    sums = dot(jnp.ones((8, g_t.shape[1]), bf16), g_t[...], (1, 1))[0:1]
    vec[...] = vec_ref[0]
    vec[7:8] = jnp.concatenate([sums, jnp.zeros((1, vec.shape[1] - 3 * part), f32)], axis=1)
    store_pieces(acc, place_ref[0], pieces[:4], pieces[4:], vec)
    add = dot(g_t[...], a_ref[0, : 3 * part, :], (0, 0))
    if last:
        gtok_out[...] = (gtok_ref[...] + add).astype(bf16)
    else:
        gtok_out[...] += add


def attend_back(first, slot, count, last, part, place, x, ga, a, qkv, ctx, lse, vec, segment, gtok):
    rows, width = x.shape
    step = width // CUBE
    return pl.pallas_call(
        functools.partial(attend_back_kernel, part, last),
        out_shape=piece_shapes(count, step, width, EXTRA) + (SDS((rows, width), bf16 if last else f32),),
        grid=(count,),
        in_specs=[
            smem_spec(),
            whole((rows, width)),
            whole((rows, width)),
            pl.BlockSpec((1, width, width), lambda i: (i + slot, 0, 0)),
            pl.BlockSpec((1, 3 * part, rows), lambda i: (i + first, 0, 0)),
            pl.BlockSpec((1, part, rows), lambda i: (i + first, 0, 0)),
            pl.BlockSpec((1, 8, rows), lambda i: (i + first, 0, 0)),
            pl.BlockSpec((1, 8, width), lambda i: (i + slot, 0, 0)),
            whole((1, rows)),
            whole((rows, width)),
        ],
        out_specs=piece_specs(step, width, EXTRA) + (whole((rows, width)),),
        scratch_shapes=[
            pltpu.VMEM((rows, rows), f32),
            pltpu.VMEM((part, rows), bf16),
            pltpu.VMEM((3 * part, rows), bf16),
            pltpu.VMEM((width, width), f32),
            pltpu.VMEM((8, width), f32),
        ],
        cost_estimate=cost(
            count * (4 * rows * width * width + 10 * rows * rows * part), count * 8e6, count * 3 * rows * rows
        ),
        name="attend_back",
    )(place, x, ga, a, qkv, ctx, lse, vec, segment, gtok)


def norm_rows(values):
    average = jnp.mean(values, -1, keepdims=True)
    centered = values - average
    spread = jnp.mean(centered * centered, -1, keepdims=True)
    rstd = lax.rsqrt(spread + EPS)
    return centered * rstd, rstd


def norm_back(grad, xhat, rstd, gain):
    scaled = grad * gain
    return rstd * (
        scaled - jnp.mean(scaled, -1, keepdims=True) - xhat * jnp.mean(scaled * xhat, -1, keepdims=True)
    )


def up_kernel(x_ref, at0, at1, vecs, u_ref, tail_ref, xhat_out, rstd_out, low_out, act_out, slope_out):
    @pl.when(pl.program_id(0) == 0)
    def _():
        attended = x_ref[...].astype(f32) + at0[...] + at1[...] + vecs[0:1]
        xhat, rstd = norm_rows(attended)
        xhat_out[...] = xhat
        rstd_out[...] = rstd
        low_out[...] = (xhat * vecs[1:2] + vecs[2:3]).astype(bf16)

    rows = x_ref.shape[0]
    chunk = 128
    bias = tail_ref[0, 1:2].astype(f32)

    def one(n, _):
        at = pl.multiple_of(n * chunk, chunk)
        pre = dot(low_out[pl.ds(at, chunk), :], u_ref[0], (1, 0)) + bias
        phi = 0.5 * (1.0 + lax.erf(pre * INV_ROOT_TWO))
        act_out[0, pl.ds(at, chunk), :] = (pre * phi).astype(bf16)
        slope_out[0, pl.ds(at, chunk), :] = (phi + pre * jnp.exp(-0.5 * pre * pre) * INV_ROOT_TWO_PI).astype(bf16)
        return 0

    lax.fori_loop(0, rows // chunk, one, 0, unroll=True)


def feed_up(x, at0, at1, vecs, u, tails):
    rows, width = x.shape
    slots, _, cols = u.shape
    full = whole((rows, width))
    return pl.pallas_call(
        up_kernel,
        out_shape=(
            SDS((rows, width), f32),
            SDS((rows, 1), f32),
            SDS((rows, width), bf16),
            SDS((slots, rows, cols), bf16),
            SDS((slots, rows, cols), bf16),
        ),
        grid=(slots,),
        in_specs=[
            full,
            full,
            full,
            whole(vecs.shape),
            pl.BlockSpec((1, width, cols), lambda i: (i, 0, 0)),
            pl.BlockSpec((1, TAIL, cols), lambda i: (i, 0, 0)),
        ],
        out_specs=(
            full,
            whole((rows, 1)),
            full,
            pl.BlockSpec((1, rows, cols), lambda i: (i, 0, 0)),
            pl.BlockSpec((1, rows, cols), lambda i: (i, 0, 0)),
        ),
        cost_estimate=cost(2 * slots * rows * width * cols, 2e7, 2 * slots * rows * cols),
        name="feed_up",
    )(x, at0, at1, vecs, u, tails)


def down_kernel(act_ref, d_ref, xhat_ref, og_ref, vecs, out_ref, gs_out, gl_out, vec_out, acc):
    i = pl.program_id(0)
    add = dot(act_ref[0], d_ref[0], (1, 0))

    @pl.when(i == 0)
    def _():
        acc[...] = xhat_ref[...] * vecs[1:2] + vecs[2:3] + vecs[3:4] + add

    @pl.when(i > 0)
    def _():
        acc[...] += add

    @pl.when(i == pl.num_programs(0) - 1)
    def _():
        xhat, rstd = norm_rows(acc[...])
        out_ref[...] = (xhat * vecs[4:5] + vecs[5:6]).astype(bf16)
        grad = og_ref[...].astype(f32)
        g_summed = norm_back(grad, xhat, rstd, vecs[4:5])
        gs_out[...] = g_summed
        gl_out[...] = g_summed.astype(bf16)
        vec_out[...] = jnp.concatenate(
            [
                jnp.sum(grad * xhat, 0, keepdims=True),
                jnp.sum(grad, 0, keepdims=True),
                jnp.sum(g_summed, 0, keepdims=True),
                jnp.zeros((5, grad.shape[1]), f32),
            ]
        )


def feed_down(act, d, xhat, og, vecs):
    slots, rows, cols = act.shape
    width = d.shape[2]
    full = whole((rows, width))
    return pl.pallas_call(
        down_kernel,
        out_shape=(
            SDS((rows, width), bf16),
            SDS((rows, width), f32),
            SDS((rows, width), bf16),
            SDS((8, width), f32),
        ),
        grid=(slots,),
        in_specs=[
            pl.BlockSpec((1, rows, cols), lambda i: (i, 0, 0)),
            pl.BlockSpec((1, cols, width), lambda i: (i, 0, 0)),
            full,
            full,
            whole(vecs.shape),
        ],
        out_specs=(full, full, full, whole((8, width))),
        scratch_shapes=[pltpu.VMEM((rows, width), f32)],
        cost_estimate=cost(2 * slots * rows * width * cols, 1.4e7, 0),
        name="feed_down",
    )(act, d, xhat, og, vecs)


def down_grad_kernel(place_ref, act_ref, gl_ref, *refs):
    pieces, acc = refs[:8], refs[8]
    acc[...] = dot(act_ref[0], gl_ref[...], (0, 0))
    store_pieces(acc, place_ref[0], pieces[:4], pieces[4:])


def down_grad(place, act, gl):
    slots, rows, cols = act.shape
    width = gl.shape[1]
    step = cols // CUBE
    return pl.pallas_call(
        down_grad_kernel,
        out_shape=piece_shapes(slots, step, width, 0),
        grid=(slots,),
        in_specs=[smem_spec(), pl.BlockSpec((1, rows, cols), lambda i: (i, 0, 0)), whole((rows, width))],
        out_specs=piece_specs(step, width, 0),
        scratch_shapes=[pltpu.VMEM((cols, width), f32)],
        cost_estimate=cost(2 * slots * rows * width * cols, 1e7, 0),
        name="down_grad",
    )(place, act, gl)


def up_grad_kernel(place_ref, gl_ref, gs_ref, low_ref, d_ref, slope_ref, u_ref, xhat_ref, rstd_ref, vecs, vec2, *refs):
    pieces, ga_out, gal_out, vec_out = refs[:8], refs[8], refs[9], refs[10]
    low_t, total, acc = refs[11:]
    i = pl.program_id(0)

    @pl.when(i == 0)
    def _():
        low_t[...] = low_ref[...].T
        vec_out[...] = jnp.zeros_like(vec_out)

    g_pre = (dot(gl_ref[...], d_ref[0], (1, 1)) * slope_ref[0].astype(f32)).astype(bf16)
    acc[...] = dot(low_t[...], g_pre, (1, 0))
    store_pieces(acc, place_ref[0], pieces[:4], pieces[4:])
    vec_out[pl.ds(i, 1), 6:7, :] = jnp.sum(g_pre.astype(f32), 0, keepdims=True)[None]
    add = dot(g_pre, u_ref[0], (1, 1))

    @pl.when(i == 0)
    def _():
        total[...] = gs_ref[...] + add

    @pl.when(i > 0)
    def _():
        total[...] += add

    @pl.when(i == pl.num_programs(0) - 1)
    def _():
        grad = total[...]
        xhat = xhat_ref[...]
        g_attended = norm_back(grad, xhat, rstd_ref[...], vecs[1:2])
        ga_out[...] = g_attended
        gal_out[...] = g_attended.astype(bf16)
        head = jnp.concatenate(
            [
                jnp.sum(grad * xhat, 0, keepdims=True),
                jnp.sum(grad, 0, keepdims=True),
                jnp.sum(g_attended, 0, keepdims=True),
                vec2[0:3],
            ]
        )
        for s in range(vec_out.shape[0]):
            vec_out[s, 0:6] = head


def up_grad(place, gl, gs, low, d, slope, u, xhat, rstd, vecs, vec2):
    slots, width, cols = u.shape
    rows = gl.shape[0]
    step = width // CUBE
    full = whole((rows, width))
    return pl.pallas_call(
        up_grad_kernel,
        out_shape=piece_shapes(slots, step, cols, 0)
        + (SDS((rows, width), f32), SDS((rows, width), bf16), SDS((slots, 8, width), f32)),
        grid=(slots,),
        in_specs=[
            smem_spec(),
            full,
            full,
            full,
            pl.BlockSpec((1, cols, width), lambda i: (i, 0, 0)),
            pl.BlockSpec((1, rows, cols), lambda i: (i, 0, 0)),
            pl.BlockSpec((1, width, cols), lambda i: (i, 0, 0)),
            full,
            whole((rows, 1)),
            whole(vecs.shape),
            whole(vec2.shape),
        ],
        out_specs=piece_specs(step, cols, 0) + (full, full, whole((slots, 8, width))),
        scratch_shapes=[
            pltpu.VMEM((width, rows), bf16),
            pltpu.VMEM((rows, width), f32),
            pltpu.VMEM((width, cols), f32),
        ],
        cost_estimate=cost(6 * slots * rows * width * cols, 2e7, 0),
        name="up_grad",
    )(place, gl, gs, low, d, slope, u, xhat, rstd, vecs, vec2)


def finish_kernel(count, step, part, place_ref, *refs):
    parts, outs, stage, sems = refs[:10], refs[10:-2], refs[-2], refs[-1]
    rows = stage.shape[1]
    copies = spread_copies(place_ref[0], parts, rows, rows, 1, lambda rel, s, first, n: stage.at[rel, pl.ds(first, n)])
    run_copies(copies, sems)
    for q in range(CUBE):
        rel = place_ref[0] ^ q
        if part:
            at = q * step
            outs[at // part][at % part : at % part + step, :] = stage[rel, 0:step].astype(f32)
            outs[4][q : q + 1, :] = stage[rel, step : step + 8].astype(f32)[0:1]
        else:
            for n in range(count):
                outs[n][q * step : (q + 1) * step, :] = stage[rel, n * step : (n + 1) * step].astype(f32)


def finish(place, parts, count, part, width):
    step = width // CUBE
    if part:
        out_shape = (SDS((part, width), f32),) * 4 + (SDS((8, width), f32),)
    else:
        out_shape = (SDS((width, width), f32),) * count
    rows = parts[0].shape[0]
    return pl.pallas_call(
        functools.partial(finish_kernel, count, step, part),
        out_shape=out_shape,
        grid=(1,),
        in_specs=[smem_spec()] + [any_spec()] * 10,
        out_specs=tuple(whole(o.shape) for o in out_shape),
        scratch_shapes=[pltpu.VMEM((CUBE, rows, width), bf16), pltpu.SemaphoreType.DMA((10,))],
        cost_estimate=cost(0, 6 * count * width * width),
        name="finish",
    )(place, *parts)


def add(*terms):
    return sum(t.astype(f32) for t in terms).astype(bf16)


def hold(*values):
    leaves, tree = jax.tree.flatten(values)
    return jax.tree.unflatten(tree, lax.optimization_barrier(leaves))


class Links:
    def __init__(self, dp, mp):
        self.dp, self.mp = dp, mp

    def shift(self, x, by):
        return lax.ppermute(x, "mp", [(i, (i + by) % self.mp) for i in range(self.mp)])

    def flip(self, x, bit):
        return lax.ppermute(x, "dp", [(i, i ^ bit) for i in range(self.dp)])

    def swap(self, values):
        return [self.flip(v, 1) for v in values]

    def across(self, x_side, y_side):
        return self.flip(x_side, 2), self.flip(y_side, 4)

    def diagonal(self, over_x, over_y):
        half = over_x.shape[0] // 16 * 8
        return self.flip(over_x[:half], 4), self.flip(over_y[half:], 2)

    def shifts(self, piece):
        return [self.shift(piece, s) for s in range(1, self.mp)]

    def total(self, terms):
        value = sum(t.astype(f32) for t in terms)
        if self.dp > CUBE:
            groups = [[g * CUBE + i for g in range(self.dp // CUBE)] for i in range(CUBE)]
            value = lax.psum(value, "dp", axis_index_groups=groups)
        return value.astype(bf16)


def by_core(pieces, received):
    return [add(keep, got) for keep, got in zip(pieces[:4], received)]


def onward(sums, from_x, from_y):
    px, py, ra, rb = sums
    return add(rb[0], from_y[0]), add(ra[0], from_x[0]), (ra[1], from_x[1]), (rb[1], from_y[1])


def landed(hop, last_x, last_y):
    own_a, own_b = add(*hop[2], last_y), add(*hop[3], last_x)
    return [jnp.concatenate([own_b[s], own_a[s]]) for s in range(own_a.shape[0])]


def per_device(
    dp,
    mp,
    tokens,
    segments,
    w_query,
    b_query,
    w_key,
    w_value,
    b_value,
    w_out,
    b_out,
    first_norm_gain,
    first_norm_bias,
    w_up,
    b_up,
    w_down,
    b_down,
    second_norm_gain,
    second_norm_bias,
    output_gradient,
):
    links = Links(dp, mp)
    rows, width = tokens.shape
    part = w_query.shape[1]
    step = width // CUBE
    here = lax.axis_index("dp") % CUBE
    place = here.astype(jnp.int32).reshape(1)
    segment = lax.dynamic_slice_in_dim(segments, lax.axis_index("mp"), 1, 0)
    vecs = jnp.concatenate(
        [b_out, first_norm_gain, first_norm_bias, b_down, second_norm_gain, second_norm_bias] + [b_out] * 2
    )
    vecs = vecs.astype(f32).reshape(8, width)

    cut = lambda block: lax.dynamic_slice_in_dim(block, here * step, step, 0)
    mixed = jnp.concatenate([w_query.T, w_key.T, w_value.T, w_out])
    zeros = jnp.zeros_like(b_query)
    tail = jnp.concatenate([b_query, zeros, b_value, zeros, b_up, jnp.zeros(((TAIL - 2) * width,), bf16)])
    tail = tail.reshape(TAIL, width)
    a_piece = jnp.concatenate([cut(mixed), tail])

    a_recv = links.shifts(a_piece)
    qkv0, ctx0, lse0, at0 = attend(0, 1, part, tokens, mixed[None], tail[None], segment)
    u_cut, d_cut = cut(w_up), cut(w_down)
    a_recv, at0, u_cut, d_cut = hold(a_recv, at0, u_cut, d_cut)

    a_cat = jnp.concatenate([t[:step] for t in a_recv])
    tails = jnp.stack([tail] + [t[step:] for t in a_recv])
    ax, ay = links.across(a_cat, a_cat)
    u_recv = links.shifts(u_cut)
    a_cat, ax, ay, u_recv, d_cut, tails = hold(a_cat, ax, ay, u_recv, d_cut, tails)

    a_diag = links.diagonal(ax, ay)
    a_odd = links.swap([a_cat, ax, ay])
    u_cat = jnp.concatenate(u_recv)
    a_diag, a_odd, u_cat = hold(a_diag, a_odd, u_cat)

    a_diag_odd = links.swap(a_diag)
    a_diag_odd, u_cat, d_cut = hold(a_diag_odd, u_cat, d_cut)

    ux, uy = links.across(u_cat, u_cat)
    d_recv = links.shifts(d_cut)
    a_all = assemble(place, mixed, [a_cat, ax, ay, *a_diag, *a_odd, *a_diag_odd], mp - 1)
    qkv1, ctx1, lse1, at1 = attend(1, mp - 1, part, tokens, a_all, tails, segment)
    ux, uy, d_recv, at1 = hold(ux, uy, d_recv, at1)

    u_diag = links.diagonal(ux, uy)
    u_odd = links.swap([u_cat, ux, uy])
    d_cat = jnp.concatenate(d_recv)
    u_diag, u_odd, d_cat = hold(u_diag, u_odd, d_cat)

    u_diag_odd = links.swap(u_diag)
    u_diag_odd, d_cat = hold(u_diag_odd, d_cat)

    dx, dy = links.across(d_cat, d_cat)
    u_all = assemble(place, w_up, [u_cat, ux, uy, *u_diag, *u_odd, *u_diag_odd], mp - 1)
    xhat1, rstd1, low, act, slope = feed_up(tokens, at0, at1, vecs, u_all, tails)
    dx, dy, act = hold(dx, dy, act)

    d_diag = links.diagonal(dx, dy)
    d_odd = links.swap([d_cat, dx, dy])
    d_diag, d_odd = hold(d_diag, d_odd)
    d_diag_odd = links.swap(d_diag)
    d_all = assemble(place, w_down, [d_cat, dx, dy, *d_diag, *d_odd, *d_diag_odd], mp - 1)
    out_tokens, g_summed, g_low, vec2 = feed_down(act, d_all, xhat1, output_gradient, vecs)

    d_pieces = down_grad(place, act, g_low)
    d_got, g_low = hold(links.swap(d_pieces[4:8]), g_low)
    d_core = by_core(d_pieces, d_got)
    d_core, g_low = hold(d_core, g_low)

    d_from = links.across(*d_core[:2])
    *u_pieces, g_att, ga_low, vec = up_grad(
        place, g_low, g_summed, low, d_all, slope, u_all, xhat1, rstd1, vecs, vec2
    )
    d_from, u_pieces, ga_low = hold(d_from, u_pieces, ga_low)

    d_hop = onward(d_core, *d_from)
    u_got, d_hop, ga_low = hold(links.swap(u_pieces[4:8]), d_hop, ga_low)
    u_core = by_core(u_pieces, u_got)
    u_core, d_hop, ga_low = hold(u_core, d_hop, ga_low)

    d_last = links.across(*d_hop[:2])
    u_from = links.across(*u_core[:2])
    half = mp // 2
    *p2, g_tok = attend_back(
        half - 1, half, mp - half, False, part, place, tokens, ga_low, a_all, qkv1, ctx1, lse1, vec, segment, g_att
    )
    d_last, u_from, p2, g_tok = hold(d_last, u_from, p2, g_tok)

    d_own = landed(d_hop, *d_last)
    u_hop = onward(u_core, *u_from)
    got2, d_own, u_hop, g_tok = hold(links.swap(p2[4:8]), d_own, u_hop, g_tok)
    core2 = by_core(p2, got2)
    core2, d_own, u_hop, g_tok = hold(core2, d_own, u_hop, g_tok)

    d_terms = [d_own[0]] + [links.shift(d_own[s], -s) for s in range(1, mp)]
    u_last = links.across(*u_hop[:2])
    from2 = links.across(*core2[:2])
    *p1, g_tok = attend_back(
        0, 1, half - 1, False, part, place, tokens, ga_low, a_all, qkv1, ctx1, lse1, vec, segment, g_tok
    )
    d_terms, u_last, from2, p1, g_tok = hold(d_terms, u_last, from2, p1, g_tok)

    d_total = links.total(d_terms)
    u_own = landed(u_hop, *u_last)
    hop2 = onward(core2, *from2)
    got1, d_total, u_own, hop2, g_tok = hold(links.swap(p1[4:8]), d_total, u_own, hop2, g_tok)
    core1 = by_core(p1, got1)
    core1, d_total, u_own, hop2, g_tok = hold(core1, d_total, u_own, hop2, g_tok)

    u_terms = [u_own[0]] + [links.shift(u_own[s], -s) for s in range(1, mp)]
    last2 = links.across(*hop2[:2])
    from1 = links.across(*core1[:2])
    *p0, g_tok = attend_back(
        0, 0, 1, True, part, place, tokens, ga_low, a_all, qkv0, ctx0, lse0, vec, segment, g_tok
    )
    u_terms, last2, from1, p0 = hold(u_terms, last2, from1, p0)

    u_total = links.total(u_terms)
    ud = jnp.concatenate([u_total, d_total])
    own2 = landed(hop2, *last2)
    hop1 = onward(core1, *from1)
    got0, ud, own2, hop1 = hold(links.swap(p0[4:8]), ud, own2, hop1)
    core0 = by_core(p0, got0)
    core0, ud, own2, hop1 = hold(core0, ud, own2, hop1)

    from0 = links.across(*core0[:2])
    last1 = links.across(*hop1[:2])
    terms2 = [links.shift(t, -(half + s)) for s, t in enumerate(own2)]
    udx, udy = links.across(ud, ud)
    from0, last1, terms2, udx, udy = hold(from0, last1, terms2, udx, udy)

    hop0 = onward(core0, *from0)
    own1 = landed(hop1, *last1)
    hop0, own1 = hold(hop0, own1)
    last0 = links.across(*hop0[:2])
    terms1 = [links.shift(t, -(1 + s)) for s, t in enumerate(own1)]
    ud_diag = links.diagonal(udx, udy)
    ud_odd = links.swap([ud, udx, udy])
    last0, terms1, ud_diag, ud_odd = hold(last0, terms1, ud_diag, ud_odd)

    a_total = links.total(landed(hop0, *last0) + terms1 + terms2)
    ud_diag_odd = links.swap(ud_diag)
    a_total, ud_diag_odd = hold(a_total, ud_diag_odd)

    tx, ty = links.across(a_total, a_total)
    g_u, g_d = finish(place, [ud, udx, udy, *ud_diag, *ud_odd, *ud_diag_odd], 2, 0, width)
    tx, ty, g_u = hold(tx, ty, g_u)
    t_diag = links.diagonal(tx, ty)
    t_odd = links.swap([a_total, tx, ty])
    t_diag_odd = links.swap(t_diag)
    g_q, g_k, g_v, g_o, v = finish(place, [a_total, tx, ty, *t_diag, *t_odd, *t_diag_odd], 1, part, width)
    return (
        out_tokens,
        g_tok,
        g_q.T,
        v[7, :part],
        g_k.T,
        g_v.T,
        v[7, 2 * part : 3 * part],
        g_o,
        v[2],
        v[0],
        v[1],
        g_u,
        v[6],
        g_d,
        v[5],
        v[3],
        v[4],
    )


def solution(mesh):
    rows, cols = P(("dp", "mp"), None), P(None, "mp")
    in_specs = (
        rows,
        P("dp", None),
        cols,
        P("mp"),
        cols,
        cols,
        P("mp"),
        P("mp", None),
        P(),
        P(),
        P(),
        cols,
        P("mp"),
        P("mp", None),
        P(),
        P(),
        P(),
        rows,
    )
    out_specs = (
        rows,
        rows,
        cols,
        P("mp"),
        cols,
        cols,
        P("mp"),
        P("mp", None),
        P(),
        P(),
        P(),
        cols,
        P("mp"),
        P("mp", None),
        P(),
        P(),
        P(),
    )
    step = functools.partial(per_device, mesh.shape["dp"], mesh.shape["mp"])
    return jax.shard_map(step, mesh=mesh, in_specs=in_specs, out_specs=out_specs, check_vma=False)
```

time: 422 us -> 334 us (0.79)
  Pallas kernels: 0 us -> 112 us
  matrix products: 74.6 us -> 0 us
  blocking collectives: 58.8 us -> 0 us
  local copies, waits for them, and re-layouts: 53.9 us -> 24.8 us
  other arithmetic: 35.9 us -> 22.3 us
  waiting for transfers between devices: 102 us -> 88.9 us
  starting transfers between devices: 87.6 us -> 77.7 us
    pallas_call x0 -> x14, Pallas kernels: none -> 112 us  [the longest x3 30.5 us: attend_back(): pl.pallas_call(functools.partial(attend_back_kernel, part, last), out_sha...]
    dot_general x72 -> x0, matrix products: 74.6 us -> none  [the longest x48 48.7 us: dot(): lax.dot_general(left, right, ((dims[:1], dims[1:]), ((), ())), preferred_...]
    psum x2 -> x0, blocking collectives: 58.8 us -> none  [the longest x1 40.9 us: per_device(): shared = lax.psum(shared, ('dp', 'mp'))]
    ppermute x24 -> x18, starting transfers between devices: 47.5 us -> 23.3 us  [shift(): lax.ppermute(x, 'mp', [(i, (i + by) % self.mp) for i in range(self.mp)])]
    ppermute x47 -> x85, waiting for transfers between devices: 76.7 us -> 55 us  [flip(): return lax.ppermute(x, 'dp', [(i, i ^ bit) for i in range(self.dp)])]
    unnamed x229 -> x181, local copies, waits for them, and re-layouts: 27.9 us -> 11.5 us
    ppermute x47 -> x85, starting transfers between devices: 40.1 us -> 54.3 us  [flip(): return lax.ppermute(x, 'dp', [(i, i ^ bit) for i in range(self.dp)])]
    concatenate x17 -> x2, local copies, waits for them, and re-layouts: 14.4 us -> 2.29 us  [the longest x1 2.1 us: per_device(): jnp.concatenate([b_query, zeros, b_value, zeros, b_up, jnp.zeros(((TAIL -...]
  transfers between devices with their start and end apart: 71 -> 103, of which waited for: 36 -> 44; matrix products, arithmetic and copies ran while one was open for 19% -> 5% of each run, Pallas kernels for 0% -> 27%
where the time goes in v2:
time: 334 us; the launch traced here: 328 us
  Pallas kernels  112 us (34%)
  waiting for transfers between devices  88.9 us (27%)
  starting transfers between devices  77.7 us (23%)
  local copies, waits for them, and re-layouts  24.8 us (7%)
  other arithmetic  22.3 us (7%)
    ppermute x85, waiting for transfers between devices, flip(): return lax.ppermute(x, 'dp', [(i, i ^ bit) for i in range(self.dp)])  55 us
    ppermute x85, starting transfers between devices, flip(): return lax.ppermute(x, 'dp', [(i, i ^ bit) for i in range(self.dp)])  54.3 us
    ppermute x18, waiting for transfers between devices, shift(): lax.ppermute(x, 'mp', [(i, (i + by) % self.mp) for i in range(self.mp)])  33.9 us
    pallas_call x3, Pallas kernels, attend_back(): pl.pallas_call(functools.partial(attend_back_kernel, part, last), out_sha...  30.5 us
    ppermute x18, starting transfers between devices, shift(): lax.ppermute(x, 'mp', [(i, (i + by) % self.mp) for i in range(self.mp)])  23.3 us
    pallas_call x2, Pallas kernels, attend(): pl.pallas_call(functools.partial(attend_kernel, part), out_shape=(SDS((co...  17.5 us
    convert_element_type x36, other arithmetic, add(): return sum((t.astype(f32) for t in terms)).astype(bf16)  16.5 us
    pallas_call x1, Pallas kernels, up_grad(): pl.pallas_call(up_grad_kernel, out_shape=piece_shapes(slots, step, cols,...  16.3 us
  transfers between devices with their start and end apart: 103, of which 44 were waited for; matrix products, arithmetic and copies ran while one was open for 5% of the time, Pallas kernels for 27%

profile of v2, /device:TPU:0, one launch (start us, length us, event | category | flops | bytes accessed | tf_op | source)
XLA Modules:
  0.0 328.1 jit_solution(7718025400718988170)
XLA Ops:
  0.7 2.1 concatenate.61
  2.9 2.4 fusion.14
  5.3 5.1 %collective-permute-start.2 = (bf16[112,768]{1,0:T(8,128)(2,1)S(1)}, bf16[112,768]{1,0:T(8,128)(2,1)S(1)}, u32[]{:S(2)}, u32[]{:S(2)}) collective-permute-start(bf16[112,768]{1,0:T(8,128)(2,1)S(1)} %pad_maximum_fusion.5), channel_id=1, source_target_pairs={{0,3},{1,0},{2,1},{3,2},{4,7},{5,4},{6,5},{7,6},{8,11},{9,8},{10,9... | collective-permute-start | bytes 516104 | tf_op jit(solution)/shard_map/ppermute | solution.py:535
  12.7 5.7 %attend.2 = (bf16[1,576,512]{2,1,0:T(8,128)(2,1)}, bf16[1,192,512]{2,1,0:T(8,128)(2,1)}, f32[1,8,512]{2,1,0:T(8,128)}, f32[512,768]{1,0:T(8,128)}) custom-call(bf16[512,768]{1,0:T(8,128)(2,1)} %x_ref.11, bf16[1,768,768]{2,1,0:T(8,128)(2,1)} %get-tuple-element.670.a_ref, bf16[1,16,768]{2,1,0:T(8,128)(2,1)} %broadcast_in_dim_reshape.3.tail_ref, ...), custom_call_target="tpu_custom_call" | custom-call | flops 805306368 | bytes 4000000 | tf_op jit(solution)/shard_map/attend/pallas_call | solution.py:127
  18.4 1.7 constant_dynamic-slice_fusion
  20.0 5.0 %collective-permute-done.1 = bf16[112,768]{1,0:T(8,128)(2,1)S(1)} collective-permute-done((bf16[112,768]{1,0:T(8,128)(2,1)S(1)}, bf16[112,768]{1,0:T(8,128)(2,1)S(1)}, u32[]{:S(2)}, u32[]{:S(2)}) %collective-permute-start.1) | collective-permute-done | bytes 172064 | tf_op jit(solution)/shard_map/ppermute | solution.py:535
  25.1 1.6 collective-permute-start.4
  29.1 1.9 collective-permute-start.6
  31.0 2.0 collective-permute-start.5
  34.2 8.9 %collective-permute-done.6 = bf16[96,768]{1,0:T(8,128)(2,1)S(1)} collective-permute-done((bf16[96,768]{1,0:T(8,128)(2,1)S(1)}, bf16[96,768]{1,0:T(8,128)(2,1)S(1)}, u32[]{:S(2)}, u32[]{:S(2)}) %collective-permute-start.6) | collective-permute-done | bytes 147488 | tf_op jit(solution)/shard_map/ppermute | solution.py:535
  45.0 6.7 %collective-permute-done.9.refs_4_ = bf16[144,768]{1,0:T(8,128)(2,1)S(1)} collective-permute-done((bf16[144,768]{1,0:T(8,128)(2,1)S(1)}, bf16[144,768]{1,0:T(8,128)(2,1)S(1)}, u32[]{:S(2)}, u32[]{:S(2)}) %collective-permute-start.9) | collective-permute-done | bytes 221216 | tf_op jit(solution)/shard_map/ppermute | solution.py:538
  57.0 2.2 collective-permute-start.17
  59.2 4.7 %assemble.3.a_ref = bf16[4,768,768]{2,1,0:T(8,128)(2,1)} custom-call(s32[1]{0:T(128)} %bitcast.7.place_ref, bf16[768,768]{1,0:T(8,128)(2,1)} %copy-done.2, bf16[288,768]{1,0:T(8,128)(2,1)} %copy-done.5, bf16[288,768]{1,0:T(8,128)(2,1)} %copy-done.10, bf16[288,768]{1,0:T(8,128)(2,1)} %copy-done.9, bf16[144,768]{1,0:T(8,128)(2,1)} %copy-done.43, ...), custom_call_target="tpu_custom_call" | custom-call | bytes 9437184 | tf_op jit(solution)/shard_map/assemble/pallas_call | solution.py:81
  63.9 11.8 %attend.3 = (bf16[3,576,512]{2,1,0:T(8,128)(2,1)}, bf16[3,192,512]{2,1,0:T(8,128)(2,1)}, f32[3,8,512]{2,1,0:T(8,128)}, f32[512,768]{1,0:T(8,128)}) custom-call(bf16[512,768]{1,0:T(8,128)(2,1)} %x_ref.11, bf16[4,768,768]{2,1,0:T(8,128)(2,1)} %assemble.3.a_ref, bf16[4,16,768]{2,1,0:T(8,128)(2,1)} %pad_maximum_fusion.17.tail_ref, ...), custom_call_target="tpu_custom_call" | custom-call | flops 2415919104 | bytes 12000000 | tf_op jit(solution)/shard_map/attend/pallas_call | solution.py:127
  77.2 1.5 collective-permute-start.20
  79.8 4.6 %collective-permute-done.21.refs_4_ = bf16[144,768]{1,0:T(8,128)(2,1)S(1)} collective-permute-done((bf16[144,768]{1,0:T(8,128)(2,1)S(1)}, bf16[144,768]{1,0:T(8,128)(2,1)S(1)}, u32[]{:S(2)}, u32[]{:S(2)}) %collective-permute-start.21) | collective-permute-done | bytes 221216 | tf_op jit(solution)/shard_map/ppermute | solution.py:538
  86.6 1.6 collective-permute-start.28
  95.1 4.7 %assemble.4.u_ref = bf16[4,768,768]{2,1,0:T(8,128)(2,1)} custom-call(s32[1]{0:T(128)} %bitcast.7.place_ref, bf16[768,768]{1,0:T(8,128)(2,1)} %own.2, bf16[288,768]{1,0:T(8,128)(2,1)} %copy-done.3, bf16[288,768]{1,0:T(8,128)(2,1)} %copy-done.8, bf16[288,768]{1,0:T(8,128)(2,1)} %copy-done.7, bf16[144,768]{1,0:T(8,128)(2,1)} %copy-done.41, ...), custom_call_target="tpu_custom_call" | custom-call | bytes 9437184 | tf_op jit(solution)/shard_map/assemble/pallas_call | solution.py:81
  99.9 9.6 %feed_up.1 = (f32[512,768]{1,0:T(8,128)}, f32[512,1]{1,0:T(8,128)}, bf16[512,768]{1,0:T(8,128)(2,1)}, bf16[4,512,768]{2,1,0:T(8,128)(2,1)}, bf16[4,512,768]{2,1,0:T(8,128)(2,1)}) custom-call(bf16[512,768]{1,0:T(8,128)(2,1)} %x_ref.11, f32[512,768]{1,0:T(8,128)} %get-tuple-element.374.at0, f32[512,768]{1,0:T(8,128)} %get-tuple-element.375.at1, ...), custom_call_target="tpu_custom_call" | custom-call | flops 2415919104 | bytes 20000000 | tf_op jit(solution)/shard_map/feed_up/pallas_call | solution.py:300
  111.4 6.6 %collective-permute-done.30.refs_4_ = bf16[144,768]{1,0:T(8,128)(2,1)S(1)} collective-permute-done((bf16[144,768]{1,0:T(8,128)(2,1)S(1)}, bf16[144,768]{1,0:T(8,128)(2,1)S(1)}, u32[]{:S(2)}, u32[]{:S(2)}) %collective-permute-start.30) | collective-permute-done | bytes 221216 | tf_op jit(solution)/shard_map/ppermute | solution.py:538
  121.2 4.7 %assemble.5.d_ref = bf16[4,768,768]{2,1,0:T(8,128)(2,1)} custom-call(s32[1]{0:T(128)} %bitcast.7.place_ref, bf16[768,768]{1,0:T(8,128)(2,1)} %own.3, bf16[288,768]{1,0:T(8,128)(2,1)} %copy-done.4, bf16[288,768]{1,0:T(8,128)(2,1)} %copy-done.12, bf16[288,768]{1,0:T(8,128)(2,1)} %copy-done.11, bf16[144,768]{1,0:T(8,128)(2,1)} %copy-done.48, ...), custom_call_target="tpu_custom_call" | custom-call | bytes 9437184 | tf_op jit(solution)/shard_map/assemble/pallas_call | solution.py:81
  125.9 9.8 %feed_down.1 = (bf16[512,768]{1,0:T(8,128)(2,1)}, f32[512,768]{1,0:T(8,128)}, bf16[512,768]{1,0:T(8,128)(2,1)}, f32[8,768]{1,0:T(8,128)}) custom-call(bf16[4,512,768]{2,1,0:T(8,128)(2,1)} %get-tuple-element.382.act_ref, bf16[4,768,768]{2,1,0:T(8,128)(2,1)} %assemble.5.d_ref, f32[512,768]{1,0:T(8,128)} %get-tuple-element.390.xhat_ref, ...), custom_call_target="tpu_custom_call" | custom-call | flops 2415919104 | bytes 14000000 | tf_op jit(solution)/shard_map/feed_down/pallas_call | solution.py:364
  135.7 7.1 %down_grad.1 = (bf16[2,4,48,768]{3,2,1,0:T(8,128)(2,1)}, bf16[2,4,48,768]{3,2,1,0:T(8,128)(2,1)}, bf16[2,4,48,768]{3,2,1,0:T(8,128)(2,1)}, bf16[2,4,48,768]{3,2,...) custom-call(s32[1]{0:T(128)} %bitcast.7.place_ref, ...), custom_call_target="tpu_custom_call" | custom-call | flops 2415919104 | bytes 10000000 | tf_op jit(solution)/shard_map/down_grad/pallas_call | solution.py:397
  150.4 1.6 collective-permute-start.40
  152.6 16.3 %up_grad.1 = (bf16[2,4,48,768]{3,2,1,0:T(8,128)(2,1)}, bf16[2,4,48,768]{3,2,1,0:T(8,128)(2,1)}, bf16[2,4,48,768]{3,2,1,0:T(8,128)(2,1)}, bf16[2,4,48,768]{3,2,1,...) custom-call(s32[1]{0:T(128)} %bitcast.7.place_ref, ...), custom_call_target="tpu_custom_call" | custom-call | flops 7247757312 | bytes 20000000 | tf_op jit(solution)/shard_map/up_grad/pallas_call | solution.py:457
  171.8 1.8 fusion
  179.2 1.6 collective-permute-start.46
  181.4 14.0 %attend_back.3 = (bf16[2,2,56,768]{3,2,1,0:T(8,128)(2,1)}, bf16[2,2,48,768]{3,2,1,0:T(8,128)(2,1)}, bf16[2,2,56,768]{3,2,1,0:T(8,128)(2,1)}, bf16[2,2,48,768]{3,...) custom-call(s32[1]{0:T(128)} %bitcast.7.place_ref, ...), custom_call_target="tpu_custom_call" | custom-call | flops 3422552064 | bytes 16000000 | tf_op jit(solution)/shard_map/attend_back/pallas_call | solution.py:226
  195.4 3.8 %collective-permute-done.46 = bf16[4,48,768]{2,1,0:T(8,128)(2,1)} collective-permute-done((bf16[4,48,768]{2,1,0:T(8,128)(2,1)}, bf16[4,48,768]{2,1,0:T(8,128)(2,1)}, u32[]{:S(2)}, u32[]{:S(2)}) %collective-permute-start.46) | collective-permute-done | bytes 294944 | tf_op jit(solution)/shard_map/ppermute | solution.py:538
  205.8 1.8 fusion.2
  209.6 1.8 collective-permute-start.54
  215.9 1.5 collective-permute-start.59
  217.5 4.4 %collective-permute-done.55 = bf16[96,768]{1,0:T(8,128)(2,1)S(1)} collective-permute-done((bf16[96,768]{1,0:T(8,128)(2,1)S(1)}, bf16[96,768]{1,0:T(8,128)(2,1)S(1)}, u32[]{:S(2)}, u32[]{:S(2)}) %collective-permute-start.55) | collective-permute-done | bytes 147488 | tf_op jit(solution)/shard_map/ppermute | solution.py:535
  223.6 8.4 %attend_back.4 = (bf16[2,1,56,768]{3,2,1,0:T(8,128)(2,1)}, bf16[2,1,48,768]{3,2,1,0:T(8,128)(2,1)}, bf16[2,1,56,768]{3,2,1,0:T(8,128)(2,1)}, bf16[2,1,48,768]{3,...) custom-call(s32[1]{0:T(128)} %bitcast.7.place_ref, ...), custom_call_target="tpu_custom_call" | custom-call | flops 1711276032 | bytes 8000000 | tf_op jit(solution)/shard_map/attend_back/pallas_call | solution.py:226
  239.7 3.2 collective-permute-start.65
  246.1 1.9 collective-permute-start.67
  248.6 8.0 %collective-permute-done.66 = bf16[96,768]{1,0:T(8,128)(2,1)S(1)} collective-permute-done((bf16[96,768]{1,0:T(8,128)(2,1)S(1)}, bf16[96,768]{1,0:T(8,128)(2,1)S(1)}, u32[]{:S(2)}, u32[]{:S(2)}) %collective-permute-start.66) | collective-permute-done | bytes 147488 | tf_op jit(solution)/shard_map/ppermute | solution.py:535
  258.1 8.1 %attend_back.5 = (bf16[2,1,56,768]{3,2,1,0:T(8,128)(2,1)}, bf16[2,1,48,768]{3,2,1,0:T(8,128)(2,1)}, bf16[2,1,56,768]{3,2,1,0:T(8,128)(2,1)}, bf16[2,1,48,768]{3,...) custom-call(s32[1]{0:T(128)} %bitcast.7.place_ref, ...), custom_call_target="tpu_custom_call" | custom-call | flops 1711276032 | bytes 8000000 | tf_op jit(solution)/shard_map/attend_back/pallas_call | solution.py:226
  270.7 1.5 collective-permute-start.82
  274.7 6.4 %collective-permute-done.78 = bf16[1,48,768]{2,1,0:T(8,128)(2,1)S(1)} collective-permute-done((bf16[1,48,768]{2,1,0:T(8,128)(2,1)S(1)}, bf16[1,48,768]{2,1,0:T(8,128)(2,1)S(1)}, u32[]{:S(2)}, u32[]{:S(2)}) %collective-permute-start.78) | collective-permute-done | bytes 73760 | tf_op jit(solution)/shard_map/ppermute | solution.py:538
  282.2 2.0 collective-permute-done.77
  285.7 6.0 %collective-permute-done.80 = bf16[104,768]{1,0:T(8,128)(2,1)S(1)} collective-permute-done((bf16[104,768]{1,0:T(8,128)(2,1)S(1)}, bf16[104,768]{1,0:T(8,128)(2,1)S(1)}, u32[]{:S(2)}, u32[]{:S(2)}) %collective-permute-start.80) | collective-permute-done | bytes 159776 | tf_op jit(solution)/shard_map/ppermute | solution.py:535
  295.9 2.5 collective-permute-done.84
  300.5 3.0 collective-permute-done.88.refs_4_
  308.0 4.1 %finish.2 = (f32[768,768]{1,0:T(8,128)}, f32[768,768]{1,0:T(8,128)}) custom-call(s32[1]{0:T(128)} %bitcast.7.place_ref, bf16[192,768]{1,0:T(8,128)(2,1)} %copy-done.6, bf16[192,768]{1,0:T(8,128)(2,1)} %copy-done.14, bf16[192,768]{1,0:T(8,128)(2,1)} %copy-done.13, bf16[96,768]{1,0:T(8,128)(2,1)} %copy-done.60, bf16[96,768]{1,0:T(8,128)(2,1)} %copy-done.59, ...), custom_call_target="tpu_custom_call" | custom-call | bytes 7077888 | tf_op jit(solution)/shard_map/finish/pallas_call | solution.py:509
  316.0 1.9 collective-permute-done.97.refs_4_
  321.9 2.9 finish.3
  326.1 1.8 slice_reduce_fusion
  (469 shorter events, 102.9 us)
Async XLA Ops:
  5.3 14.7 %collective-permute-start.2 = (bf16[112,768]{1,0:T(8,128)(2,1)S(1)}, bf16[112,768]{1,0:T(8,128)(2,1)S(1)}, u32[]{:S(2)}, u32[]{:S(2)}) collective-permute-start(bf16[112,768]{1,0:T(8,128)(2,1)S(1)} %pad_maximum_fusion.5), channel_id=1, source_target_pairs={{0,3},{1,0},{2,1},{3,2},{4,7},{5,4},{6,5},{7,6},{8,11},{9,8},{10,9... | collective-permute-start | bytes 516104 | tf_op jit(solution)/shard_map/ppermute | solution.py:535
  10.4 14.6 %collective-permute-start.1 = (bf16[112,768]{1,0:T(8,128)(2,1)S(1)}, bf16[112,768]{1,0:T(8,128)(2,1)S(1)}, u32[]{:S(2)}, u32[]{:S(2)}) collective-permute-start(bf16[112,768]{1,0:T(8,128)(2,1)S(1)} %pad_maximum_fusion.5), channel_id=1, source_target_pairs={{0,2},{1,3},{2,0},{3,1},{4,6},{5,7},{6,4},{7,5},{8,10},{9,11},{10,... | collective-permute-start | bytes 516104 | tf_op jit(solution)/shard_map/ppermute | solution.py:535
  10.4 14.6 %collective-permute-start = (bf16[112,768]{1,0:T(8,128)(2,1)S(1)}, bf16[112,768]{1,0:T(8,128)(2,1)S(1)}, u32[]{:S(2)}, u32[]{:S(2)}) collective-permute-start(bf16[112,768]{1,0:T(8,128)(2,1)S(1)} %pad_maximum_fusion.5), channel_id=1, source_target_pairs={{0,1},{1,2},{2,3},{3,0},{4,5},{5,6},{6,7},{7,4},{8,9},{9,10},{10,1... | collective-permute-start | bytes 516104 | tf_op jit(solution)/shard_map/ppermute | solution.py:535
  25.1 18.0 %collective-permute-start.4 = (bf16[288,768]{1,0:T(8,128)(2,1)S(1)}, bf16[288,768]{1,0:T(8,128)(2,1)S(1)}, u32[]{:S(2)}, u32[]{:S(2)}) collective-permute-start(bf16[288,768]{1,0:T(8,128)(2,1)S(1)} %pad_maximum_fusion.1.refs_0_), channel_id=1, source_target_pairs={{0,16},{4,20},{8,24},{12,28},{16,0},{20,4},{24,8},{28,12},{1,17},{... | collective-permute-start | bytes 1327112 | tf_op jit(solution)/shard_map/ppermute | solution.py:538
  26.7 16.5 %collective-permute-start.3 = (bf16[288,768]{1,0:T(8,128)(2,1)S(1)}, bf16[288,768]{1,0:T(8,128)(2,1)S(1)}, u32[]{:S(2)}, u32[]{:S(2)}) collective-permute-start(bf16[288,768]{1,0:T(8,128)(2,1)S(1)} %pad_maximum_fusion.1.refs_0_), channel_id=1, source_target_pairs={{0,8},{4,12},{8,0},{12,4},{16,24},{20,28},{24,16},{28,20},{1,9},{5... | collective-permute-start | bytes 1327112 | tf_op jit(solution)/shard_map/ppermute | solution.py:538
  29.1 14.1 %collective-permute-start.6 = (bf16[96,768]{1,0:T(8,128)(2,1)S(1)}, bf16[96,768]{1,0:T(8,128)(2,1)S(1)}, u32[]{:S(2)}, u32[]{:S(2)}) collective-permute-start(bf16[96,768]{1,0:T(8,128)(2,1)S(1)} %get-tuple-element.344), channel_id=1, source_target_pairs={{0,2},{1,3},{2,0},{3,1},{4,6},{5,7},{6,4},{7,5},{8,10},{9,11},{10,... | collective-permute-start | bytes 442376 | tf_op jit(solution)/shard_map/ppermute | solution.py:535
  31.0 12.2 %collective-permute-start.5 = (bf16[96,768]{1,0:T(8,128)(2,1)S(1)}, bf16[96,768]{1,0:T(8,128)(2,1)S(1)}, u32[]{:S(2)}, u32[]{:S(2)}) collective-permute-start(bf16[96,768]{1,0:T(8,128)(2,1)S(1)} %get-tuple-element.344), channel_id=1, source_target_pairs={{0,1},{1,2},{2,3},{3,0},{4,5},{5,6},{6,7},{7,4},{8,9},{9,10},{10,1... | collective-permute-start | bytes 442376 | tf_op jit(solution)/shard_map/ppermute | solution.py:535
  43.2 8.8 %collective-permute-start.10 = (bf16[288,768]{1,0:T(8,128)(2,1)S(1)}, bf16[288,768]{1,0:T(8,128)(2,1)S(1)}, u32[]{:S(2)}, u32[]{:S(2)}) collective-permute-start(bf16[288,768]{1,0:T(8,128)(2,1)S(1)} %pad_maximum_fusion.1.refs_0_), channel_id=1, source_target_pairs={{0,4},{4,0},{8,12},{12,8},{16,20},{20,16},{24,28},{28,24},{1,5},{5... | collective-permute-start | bytes 1327112 | tf_op jit(solution)/shard_map/ppermute | solution.py:538
  43.3 8.7 %collective-permute-start.11 = (bf16[288,768]{1,0:T(8,128)(2,1)S(1)}, bf16[288,768]{1,0:T(8,128)(2,1)S(1)}, u32[]{:S(2)}, u32[]{:S(2)}) collective-permute-start(bf16[288,768]{1,0:T(8,128)(2,1)S(1)} %collective-permute-done.3.refs_1_), channel_id=1, source_target_pairs={{0,4},{4,0},{8,12},{12,8},{16,20},{20,16},{24,28},{28,24},{1,5},{5... | collective-permute-start | bytes 1327112 | tf_op jit(solution)/shard_map/ppermute | solution.py:538
  53.9 22.0 %collective-permute-start.16 = (bf16[288,768]{1,0:T(8,128)(2,1)S(1)}, bf16[288,768]{1,0:T(8,128)(2,1)S(1)}, u32[]{:S(2)}, u32[]{:S(2)}) collective-permute-start(bf16[288,768]{1,0:T(8,128)(2,1)S(1)} %pad_maximum_fusion.2.refs_0_), channel_id=1, source_target_pairs={{0,16},{4,20},{8,24},{12,28},{16,0},{20,4},{24,8},{28,12},{1,17},{... | collective-permute-start | bytes 1327112 | tf_op jit(solution)/shard_map/ppermute | solution.py:538
  54.5 21.4 %collective-permute-start.15 = (bf16[288,768]{1,0:T(8,128)(2,1)S(1)}, bf16[288,768]{1,0:T(8,128)(2,1)S(1)}, u32[]{:S(2)}, u32[]{:S(2)}) collective-permute-start(bf16[288,768]{1,0:T(8,128)(2,1)S(1)} %pad_maximum_fusion.2.refs_0_), channel_id=1, source_target_pairs={{0,8},{4,12},{8,0},{12,4},{16,24},{20,28},{24,16},{28,20},{1,9},{5... | collective-permute-start | bytes 1327112 | tf_op jit(solution)/shard_map/ppermute | solution.py:538
  56.0 19.8 %collective-permute-start.19 = (bf16[96,768]{1,0:T(8,128)(2,1)}, bf16[96,768]{1,0:T(8,128)(2,1)}, u32[]{:S(2)}, u32[]{:S(2)}) collective-permute-start(bf16[96,768]{1,0:T(8,128)(2,1)} %get-tuple-element.357), channel_id=1, source_target_pairs={{0,3},{1,0},{2,1},{3,2},{4,7},{5,4},{6,5},{7,6},{8,11},{9,8},{10,9... | collective-permute-start | bytes 442376 | tf_op jit(solution)/shard_map/ppermute | solution.py:535
  56.0 19.9 %collective-permute-start.18 = (bf16[96,768]{1,0:T(8,128)(2,1)}, bf16[96,768]{1,0:T(8,128)(2,1)}, u32[]{:S(2)}, u32[]{:S(2)}) collective-permute-start(bf16[96,768]{1,0:T(8,128)(2,1)} %get-tuple-element.357), channel_id=1, source_target_pairs={{0,2},{1,3},{2,0},{3,1},{4,6},{5,7},{6,4},{7,5},{8,10},{9,11},{10,... | collective-permute-start | bytes 442376 | tf_op jit(solution)/shard_map/ppermute | solution.py:535
  57.0 18.8 %collective-permute-start.17 = (bf16[96,768]{1,0:T(8,128)(2,1)}, bf16[96,768]{1,0:T(8,128)(2,1)}, u32[]{:S(2)}, u32[]{:S(2)}) collective-permute-start(bf16[96,768]{1,0:T(8,128)(2,1)} %get-tuple-element.357), channel_id=1, source_target_pairs={{0,1},{1,2},{2,3},{3,0},{4,5},{5,6},{6,7},{7,4},{8,9},{9,10},{10,1... | collective-permute-start | bytes 442376 | tf_op jit(solution)/shard_map/ppermute | solution.py:535
  75.9 8.8 %collective-permute-start.23 = (bf16[288,768]{1,0:T(8,128)(2,1)S(1)}, bf16[288,768]{1,0:T(8,128)(2,1)S(1)}, u32[]{:S(2)}, u32[]{:S(2)}) collective-permute-start(bf16[288,768]{1,0:T(8,128)(2,1)S(1)} %collective-permute-done.15.refs_1_), channel_id=1, source_target_pairs={{0,4},{4,0},{8,12},{12,8},{16,20},{20,16},{24,28},{28,24},{1,5},{5... | collective-permute-start | bytes 1327112 | tf_op jit(solution)/shard_map/ppermute | solution.py:538
  86.6 22.9 %collective-permute-start.28 = (bf16[288,768]{1,0:T(8,128)(2,1)S(1)}, bf16[288,768]{1,0:T(8,128)(2,1)S(1)}, u32[]{:S(2)}, u32[]{:S(2)}) collective-permute-start(bf16[288,768]{1,0:T(8,128)(2,1)S(1)} %pad_maximum_fusion.3.refs_0_), channel_id=1, source_target_pairs={{0,16},{4,20},{8,24},{12,28},{16,0},{20,4},{24,8},{28,12},{1,17},{... | collective-permute-start | bytes 1327112 | tf_op jit(solution)/shard_map/ppermute | solution.py:538
  88.1 21.3 %collective-permute-start.27 = (bf16[288,768]{1,0:T(8,128)(2,1)S(1)}, bf16[288,768]{1,0:T(8,128)(2,1)S(1)}, u32[]{:S(2)}, u32[]{:S(2)}) collective-permute-start(bf16[288,768]{1,0:T(8,128)(2,1)S(1)} %pad_maximum_fusion.3.refs_0_), channel_id=1, source_target_pairs={{0,8},{4,12},{8,0},{12,4},{16,24},{20,28},{24,16},{28,20},{1,9},{5... | collective-permute-start | bytes 1327112 | tf_op jit(solution)/shard_map/ppermute | solution.py:538
  95.1 16.3 %collective-permute-start.31 = (bf16[288,768]{1,0:T(8,128)(2,1)S(1)}, bf16[288,768]{1,0:T(8,128)(2,1)}, u32[]{:S(2)}, u32[]{:S(2)}) collective-permute-start(bf16[288,768]{1,0:T(8,128)(2,1)S(1)} %pad_maximum_fusion.3.refs_0_), channel_id=1, source_target_pairs={{0,4},{4,0},{8,12},{12,8},{16,20},{20,16},{24,28},{28,24},{1,5},{5... | collective-permute-start | bytes 1327112 | tf_op jit(solution)/shard_map/ppermute | solution.py:538
  109.5 8.8 %collective-permute-start.32 = (bf16[288,768]{1,0:T(8,128)(2,1)S(1)}, bf16[288,768]{1,0:T(8,128)(2,1)S(1)}, u32[]{:S(2)}, u32[]{:S(2)}) collective-permute-start(bf16[288,768]{1,0:T(8,128)(2,1)S(1)} %collective-permute-done.27.refs_1_), channel_id=1, source_target_pairs={{0,4},{4,0},{8,12},{12,8},{16,20},{20,16},{24,28},{28,24},{1,5},{5... | collective-permute-start | bytes 1327112 | tf_op jit(solution)/shard_map/ppermute | solution.py:538
  150.4 18.5 %collective-permute-start.40 = (bf16[2,4,48,768]{3,2,1,0:T(8,128)(2,1)S(1)}, bf16[2,4,48,768]{3,2,1,0:T(8,128)(2,1)S(1)}, u32[]{:S(2)}, u32[]{:S(2)}) collective-permute-start(bf16[2,4,48,768]{3,2,1,0:T(8,128)(2,1)S(1)} %add_convert_fusion.7), channel_id=1, source_target_pairs={{0,8},{4,12},{8,0},{12,4},{16,24},{20,28},{24,16},{28,20},{1,9},{5... | collective-permute-start | bytes 1769480 | tf_op jit(solution)/shard_map/ppermute | solution.py:538
  151.9 17.0 %collective-permute-start.41 = (bf16[2,4,48,768]{3,2,1,0:T(8,128)(2,1)S(1)}, bf16[2,4,48,768]{3,2,1,0:T(8,128)(2,1)}, u32[]{:S(2)}, u32[]{:S(2)}) collective-permute-start(bf16[2,4,48,768]{3,2,1,0:T(8,128)(2,1)S(1)} %add_convert_fusion.6), channel_id=1, source_target_pairs={{0,16},{4,20},{8,24},{12,28},{16,0},{20,4},{24,8},{28,12},{1,17},{... | collective-permute-start | bytes 1769480 | tf_op jit(solution)/shard_map/ppermute | solution.py:538
  177.2 22.1 %collective-permute-start.48 = (bf16[2,4,48,768]{3,2,1,0:T(8,128)(2,1)}, bf16[2,4,48,768]{3,2,1,0:T(8,128)(2,1)}, u32[]{:S(2)}, u32[]{:S(2)}) collective-permute-start(bf16[2,4,48,768]{3,2,1,0:T(8,128)(2,1)} %add_convert_fusion.3), channel_id=1, source_target_pairs={{0,8},{4,12},{8,0},{12,4},{16,24},{20,28},{24,16},{28,20},{1,9},{5... | collective-permute-start | bytes 1769480 | tf_op jit(solution)/shard_map/ppermute | solution.py:538
  177.8 21.5 %collective-permute-start.49 = (bf16[2,4,48,768]{3,2,1,0:T(8,128)(2,1)S(1)}, bf16[2,4,48,768]{3,2,1,0:T(8,128)(2,1)}, u32[]{:S(2)}, u32[]{:S(2)}) collective-permute-start(bf16[2,4,48,768]{3,2,1,0:T(8,128)(2,1)S(1)} %add_convert_fusion.2), channel_id=1, source_target_pairs={{0,16},{4,20},{8,24},{12,28},{16,0},{20,4},{24,8},{28,12},{1,17},{... | collective-permute-start | bytes 1769480 | tf_op jit(solution)/shard_map/ppermute | solution.py:538
  179.2 20.1 %collective-permute-start.46 = (bf16[4,48,768]{2,1,0:T(8,128)(2,1)}, bf16[4,48,768]{2,1,0:T(8,128)(2,1)}, u32[]{:S(2)}, u32[]{:S(2)}) collective-permute-start(bf16[4,48,768]{2,1,0:T(8,128)(2,1)} %fusion), channel_id=1, source_target_pairs={{0,8},{4,12},{8,0},{12,4},{16,24},{20,28},{24,16},{28,20},{1,9},{5... | collective-permute-start | bytes 884744 | tf_op jit(solution)/shard_map/ppermute | solution.py:538
  180.7 18.5 %collective-permute-start.47 = (bf16[4,48,768]{2,1,0:T(8,128)(2,1)}, bf16[4,48,768]{2,1,0:T(8,128)(2,1)}, u32[]{:S(2)}, u32[]{:S(2)}) collective-permute-start(bf16[4,48,768]{2,1,0:T(8,128)(2,1)} %fusion.1), channel_id=1, source_target_pairs={{0,16},{4,20},{8,24},{12,28},{16,0},{20,4},{24,8},{28,12},{1,17},{... | collective-permute-start | bytes 884744 | tf_op jit(solution)/shard_map/ppermute | solution.py:538
  211.4 10.5 %collective-permute-start.55 = (bf16[96,768]{1,0:T(8,128)(2,1)S(1)}, bf16[96,768]{1,0:T(8,128)(2,1)S(1)}, u32[]{:S(2)}, u32[]{:S(2)}) collective-permute-start(bf16[96,768]{1,0:T(8,128)(2,1)S(1)} %pad_maximum_fusion.11), channel_id=1, source_target_pairs={{0,2},{1,3},{2,0},{3,1},{4,6},{5,7},{6,4},{7,5},{8,10},{9,11},{10,... | collective-permute-start | bytes 442376 | tf_op jit(solution)/shard_map/ppermute | solution.py:535
  211.4 20.6 %collective-permute-start.57 = (bf16[4,48,768]{2,1,0:T(8,128)(2,1)}, bf16[4,48,768]{2,1,0:T(8,128)(2,1)}, u32[]{:S(2)}, u32[]{:S(2)}) collective-permute-start(bf16[4,48,768]{2,1,0:T(8,128)(2,1)} %fusion.2), channel_id=1, source_target_pairs={{0,8},{4,12},{8,0},{12,4},{16,24},{20,28},{24,16},{28,20},{1,9},{5... | collective-permute-start | bytes 884744 | tf_op jit(solution)/shard_map/ppermute | solution.py:538
  212.9 19.1 %collective-permute-start.58 = (bf16[4,48,768]{2,1,0:T(8,128)(2,1)S(1)}, bf16[4,48,768]{2,1,0:T(8,128)(2,1)}, u32[]{:S(2)}, u32[]{:S(2)}) collective-permute-start(bf16[4,48,768]{2,1,0:T(8,128)(2,1)S(1)} %fusion.3), channel_id=1, source_target_pairs={{0,16},{4,20},{8,24},{12,28},{16,0},{20,4},{24,8},{28,12},{1,17},{... | collective-permute-start | bytes 884744 | tf_op jit(solution)/shard_map/ppermute | solution.py:538
  214.3 17.7 %collective-permute-start.60 = (bf16[2,2,48,768]{3,2,1,0:T(8,128)(2,1)}, bf16[2,2,48,768]{3,2,1,0:T(8,128)(2,1)}, u32[]{:S(2)}, u32[]{:S(2)}) collective-permute-start(bf16[2,2,48,768]{3,2,1,0:T(8,128)(2,1)} %add_convert_fusion.13), channel_id=1, source_target_pairs={{0,16},{4,20},{8,24},{12,28},{16,0},{20,4},{24,8},{28,12},{1,17},{... | collective-permute-start | bytes 884744 | tf_op jit(solution)/shard_map/ppermute | solution.py:538
  215.9 16.2 %collective-permute-start.59 = (bf16[2,2,56,768]{3,2,1,0:T(8,128)(2,1)S(1)}, bf16[2,2,56,768]{3,2,1,0:T(8,128)(2,1)S(1)}, u32[]{:S(2)}, u32[]{:S(2)}) collective-permute-start(bf16[2,2,56,768]{3,2,1,0:T(8,128)(2,1)S(1)} %add_convert_fusion.9), channel_id=1, source_target_pairs={{0,8},{4,12},{8,0},{12,4},{16,24},{20,28},{24,16},{28,20},{1,9},{5... | collective-permute-start | bytes 1032200 | tf_op jit(solution)/shard_map/ppermute | solution.py:538
  222.6 9.5 %collective-permute-start.56 = (bf16[96,768]{1,0:T(8,128)(2,1)S(1)}, bf16[96,768]{1,0:T(8,128)(2,1)}, u32[]{:S(2)}, u32[]{:S(2)}) collective-permute-start(bf16[96,768]{1,0:T(8,128)(2,1)S(1)} %pad_maximum_fusion.12), channel_id=1, source_target_pairs={{0,1},{1,2},{2,3},{3,0},{4,5},{5,6},{6,7},{7,4},{8,9},{9,10},{10,1... | collective-permute-start | bytes 442376 | tf_op jit(solution)/shard_map/ppermute | solution.py:535
  239.7 8.4 %collective-permute-start.65 = (bf16[96,768]{1,0:T(8,128)(2,1)S(1)}, bf16[96,768]{1,0:T(8,128)(2,1)S(1)}, u32[]{:S(2)}, u32[]{:S(2)}) collective-permute-start(bf16[96,768]{1,0:T(8,128)(2,1)S(1)} %pad_maximum_fusion.14), channel_id=1, source_target_pairs={{0,3},{1,0},{2,1},{3,2},{4,7},{5,4},{6,5},{7,6},{8,11},{9,8},{10,9... | collective-permute-start | bytes 442376 | tf_op jit(solution)/shard_map/ppermute | solution.py:535
  242.9 13.8 %collective-permute-start.66 = (bf16[96,768]{1,0:T(8,128)(2,1)S(1)}, bf16[96,768]{1,0:T(8,128)(2,1)S(1)}, u32[]{:S(2)}, u32[]{:S(2)}) collective-permute-start(bf16[96,768]{1,0:T(8,128)(2,1)S(1)} %pad_maximum_fusion.15), channel_id=1, source_target_pairs={{0,2},{1,3},{2,0},{3,1},{4,6},{5,7},{6,4},{7,5},{8,10},{9,11},{10,... | collective-permute-start | bytes 442376 | tf_op jit(solution)/shard_map/ppermute | solution.py:535
  243.2 23.0 %collective-permute-start.69 = (bf16[2,56,768]{2,1,0:T(8,128)(2,1)S(1)}, bf16[2,56,768]{2,1,0:T(8,128)(2,1)S(1)}, u32[]{:S(2)}, u32[]{:S(2)}) collective-permute-start(bf16[2,56,768]{2,1,0:T(8,128)(2,1)S(1)} %fusion.4), channel_id=1, source_target_pairs={{0,16},{4,20},{8,24},{12,28},{16,0},{20,4},{24,8},{28,12},{1,17},{... | collective-permute-start | bytes 516104 | tf_op jit(solution)/shard_map/ppermute | solution.py:538
  244.6 21.6 %collective-permute-start.70 = (bf16[2,1,56,768]{3,2,1,0:T(8,128)(2,1)S(1)}, bf16[2,1,56,768]{3,2,1,0:T(8,128)(2,1)S(1)}, u32[]{:S(2)}, u32[]{:S(2)}) collective-permute-start(bf16[2,1,56,768]{3,2,1,0:T(8,128)(2,1)S(1)} %add_convert_fusion.24), channel_id=1, source_target_pairs={{0,8},{4,12},{8,0},{12,4},{16,24},{20,28},{24,16},{28,20},{1,9},{5... | collective-permute-start | bytes 516104 | tf_op jit(solution)/shard_map/ppermute | solution.py:538
  246.1 20.1 %collective-permute-start.67 = (bf16[96,768]{1,0:T(8,128)(2,1)S(1)}, bf16[96,768]{1,0:T(8,128)(2,1)S(1)}, u32[]{:S(2)}, u32[]{:S(2)}) collective-permute-start(bf16[96,768]{1,0:T(8,128)(2,1)S(1)} %pad_maximum_fusion.16), channel_id=1, source_target_pairs={{0,1},{1,2},{2,3},{3,0},{4,5},{5,6},{6,7},{7,4},{8,9},{9,10},{10,1... | collective-permute-start | bytes 442376 | tf_op jit(solution)/shard_map/ppermute | solution.py:535
  248.0 18.1 %collective-permute-start.68 = (bf16[2,48,768]{2,1,0:T(8,128)(2,1)S(1)}, bf16[2,48,768]{2,1,0:T(8,128)(2,1)}, u32[]{:S(2)}, u32[]{:S(2)}) collective-permute-start(bf16[2,48,768]{2,1,0:T(8,128)(2,1)S(1)} %fusion.5), channel_id=1, source_target_pairs={{0,8},{4,12},{8,0},{12,4},{16,24},{20,28},{24,16},{28,20},{1,9},{5... | collective-permute-start | bytes 442376 | tf_op jit(solution)/shard_map/ppermute | solution.py:538
  256.7 9.5 %collective-permute-start.71 = (bf16[2,1,48,768]{3,2,1,0:T(8,128)(2,1)S(1)}, bf16[2,1,48,768]{3,2,1,0:T(8,128)(2,1)S(1)}, u32[]{:S(2)}, u32[]{:S(2)}) collective-permute-start(bf16[2,1,48,768]{3,2,1,0:T(8,128)(2,1)S(1)} %add_convert_fusion.32), channel_id=1, source_target_pairs={{0,16},{4,20},{8,24},{12,28},{16,0},{20,4},{24,8},{28,12},{1,17},{... | collective-permute-start | bytes 442376 | tf_op jit(solution)/shard_map/ppermute | solution.py:538
  270.0 21.8 %collective-permute-start.83 = (bf16[192,768]{1,0:T(8,128)(2,1)S(1)}, bf16[192,768]{1,0:T(8,128)(2,1)S(1)}, u32[]{:S(2)}, u32[]{:S(2)}) collective-permute-start(bf16[192,768]{1,0:T(8,128)(2,1)S(1)} %pad_maximum_fusion.4.refs_0_), channel_id=1, source_target_pairs={{0,16},{4,20},{8,24},{12,28},{16,0},{20,4},{24,8},{28,12},{1,17},{... | collective-permute-start | bytes 884744 | tf_op jit(solution)/shard_map/ppermute | solution.py:538
  270.7 21.1 %collective-permute-start.82 = (bf16[192,768]{1,0:T(8,128)(2,1)S(1)}, bf16[192,768]{1,0:T(8,128)(2,1)S(1)}, u32[]{:S(2)}, u32[]{:S(2)}) collective-permute-start(bf16[192,768]{1,0:T(8,128)(2,1)S(1)} %pad_maximum_fusion.4.refs_0_), channel_id=1, source_target_pairs={{0,8},{4,12},{8,0},{12,4},{16,24},{20,28},{24,16},{28,20},{1,9},{5... | collective-permute-start | bytes 884744 | tf_op jit(solution)/shard_map/ppermute | solution.py:538
  272.2 9.0 %collective-permute-start.78 = (bf16[1,48,768]{2,1,0:T(8,128)(2,1)S(1)}, bf16[1,48,768]{2,1,0:T(8,128)(2,1)S(1)}, u32[]{:S(2)}, u32[]{:S(2)}) collective-permute-start(bf16[1,48,768]{2,1,0:T(8,128)(2,1)S(1)} %fusion.10), channel_id=1, source_target_pairs={{0,8},{4,12},{8,0},{12,4},{16,24},{20,28},{24,16},{28,20},{1,9},{5... | collective-permute-start | bytes 221192 | tf_op jit(solution)/shard_map/ppermute | solution.py:538
  272.7 9.0 %collective-permute-start.79 = (bf16[1,56,768]{2,1,0:T(8,128)(2,1)S(1)}, bf16[1,56,768]{2,1,0:T(8,128)(2,1)S(1)}, u32[]{:S(2)}, u32[]{:S(2)}) collective-permute-start(bf16[1,56,768]{2,1,0:T(8,128)(2,1)S(1)} %fusion.6), channel_id=1, source_target_pairs={{0,16},{4,20},{8,24},{12,28},{16,0},{20,4},{24,8},{28,12},{1,17},{... | collective-permute-start | bytes 258056 | tf_op jit(solution)/shard_map/ppermute | solution.py:538
  274.1 10.1 %collective-permute-start.77 = (bf16[2,1,48,768]{3,2,1,0:T(8,128)(2,1)S(1)}, bf16[2,1,48,768]{3,2,1,0:T(8,128)(2,1)S(1)}, u32[]{:S(2)}, u32[]{:S(2)}) collective-permute-start(bf16[2,1,48,768]{3,2,1,0:T(8,128)(2,1)S(1)} %add_convert_fusion.28), channel_id=1, source_target_pairs={{0,16},{4,20},{8,24},{12,28},{16,0},{20,4},{24,8},{28,12},{1,17},{... | collective-permute-start | bytes 442376 | tf_op jit(solution)/shard_map/ppermute | solution.py:538
  281.2 10.6 %collective-permute-start.80 = (bf16[104,768]{1,0:T(8,128)(2,1)S(1)}, bf16[104,768]{1,0:T(8,128)(2,1)S(1)}, u32[]{:S(2)}, u32[]{:S(2)}) collective-permute-start(bf16[104,768]{1,0:T(8,128)(2,1)S(1)} %pad_maximum_fusion.6), channel_id=1, source_target_pairs={{0,2},{1,3},{2,0},{3,1},{4,6},{5,7},{6,4},{7,5},{8,10},{9,11},{10,... | collective-permute-start | bytes 479240 | tf_op jit(solution)/shard_map/ppermute | solution.py:535
  281.7 10.0 %collective-permute-start.81 = (bf16[104,768]{1,0:T(8,128)(2,1)S(1)}, bf16[104,768]{1,0:T(8,128)(2,1)S(1)}, u32[]{:S(2)}, u32[]{:S(2)}) collective-permute-start(bf16[104,768]{1,0:T(8,128)(2,1)S(1)} %pad_maximum_fusion.7), channel_id=1, source_target_pairs={{0,1},{1,2},{2,3},{3,0},{4,5},{5,6},{6,7},{7,4},{8,9},{9,10},{10,1... | collective-permute-start | bytes 479240 | tf_op jit(solution)/shard_map/ppermute | solution.py:535
  291.9 13.1 %collective-permute-start.90 = (bf16[192,768]{1,0:T(8,128)(2,1)S(1)}, bf16[192,768]{1,0:T(8,128)(2,1)S(1)}, u32[]{:S(2)}, u32[]{:S(2)}) collective-permute-start(bf16[192,768]{1,0:T(8,128)(2,1)S(1)} %collective-permute-done.82.refs_1_), channel_id=1, source_target_pairs={{0,4},{4,0},{8,12},{12,8},{16,20},{20,16},{24,28},{28,24},{1,5},{5... | collective-permute-start | bytes 884744 | tf_op jit(solution)/shard_map/ppermute | solution.py:538
  292.5 12.6 %collective-permute-start.91 = (bf16[192,768]{1,0:T(8,128)(2,1)S(1)}, bf16[192,768]{1,0:T(8,128)(2,1)S(1)}, u32[]{:S(2)}, u32[]{:S(2)}) collective-permute-start(bf16[192,768]{1,0:T(8,128)(2,1)S(1)} %collective-permute-done.83.refs_2_), channel_id=1, source_target_pairs={{0,4},{4,0},{8,12},{12,8},{16,20},{20,16},{24,28},{28,24},{1,5},{5... | collective-permute-start | bytes 884744 | tf_op jit(solution)/shard_map/ppermute | solution.py:538
  295.5 9.5 %collective-permute-start.86 = (bf16[104,768]{1,0:T(8,128)(2,1)S(1)}, bf16[104,768]{1,0:T(8,128)(2,1)S(1)}, u32[]{:S(2)}, u32[]{:S(2)}) collective-permute-start(bf16[104,768]{1,0:T(8,128)(2,1)S(1)} %pad_maximum_fusion.8), channel_id=1, source_target_pairs={{0,3},{1,0},{2,1},{3,2},{4,7},{5,4},{6,5},{7,6},{8,11},{9,8},{10,9... | collective-permute-start | bytes 479240 | tf_op jit(solution)/shard_map/ppermute | solution.py:535
  (142 other events, 728.0 us)
